TPU v7x, 256 devices: a whole 4x4x8 slice. The times are simulated.
256 devices in a mesh: seq: 32 (over x, z), head: 8 (over y, core).
Axes of the slice: x: 4, y: 4, z: 8, core: 2. Of those that a mesh axis runs over, the one named last changes fastest.
Arguments:
- query_projection: bfloat16 [8192, 4096], P(('seq', 'head')), may hold values from -6 to 6
- key_projection: bfloat16 [8192, 1024], P(('seq', 'head')), may hold values from -6 to 6
- value_projection: bfloat16 [8192, 1024], P(('seq', 'head')), may hold values from -6 to 6
- output_gradient: bfloat16 [8192, 4096], P(('seq', 'head')), may hold values from -6 to 6
- partners: int32 [64, 6], P('seq'), may hold values from -1 to 62, as said below
Outputs:
- attention: bfloat16 [8192, 4096], P('seq', 'head')
- grad_query: bfloat16 [8192, 4096], P('seq', 'head')
- key_gradient: bfloat16 [8192, 1024], P('seq', 'head')
- value_gradient: bfloat16 [8192, 1024], P('seq', 'head')
Inputs may be any that keep to these rules, and one draw needn't show every extreme that they name: For l < 1, partners[b, l] is -1 if b < 2**l, else a block at a distance of 2**l to 2**(l+1) - 1 blocks before b (not before block 0). For l = 1 + j, with g = b // 2 - 2**j, it is -1 if g < 0, else one of the blocks g * 2 to g * 2 + 1.
All inputs are finite; a program needn't handle non-finite values.
Results may differ from a plain program's by a relative error of at most 0.012.
Values may be sent and summed in bfloat16 or wider, within the bound.
No kernel may reach another device: no remote copies, remote signals or barrier semaphores. Data moves between devices by JAX's collectives and lax.ppermute only.
A program may use at most 64 MiB of HBM per device.

v0:
```python
import math

import jax
import jax.numpy as jnp
from jax import lax
from jax.sharding import PartitionSpec as P

HEAD_SIZE = 128
BLOCK_TOKENS = 128


masked_score = -1e30


def from_behind(value, axis, steps):
    count = lax.axis_size(axis)
    initial, last = (max(0, -steps), min(count, count - steps))
    return lax.ppermute(value, axis, [(source, source + steps) for source in range(initial, last)])


def shards(query_projection, key_projection, value_projection, output_gradient, partners):
    q_local, dout_local, k_local, v_local = (
        lax.all_to_all(query_projection, "head", split_axis=1, concat_axis=0, tiled=True),
        lax.all_to_all(output_gradient, "head", split_axis=1, concat_axis=0, tiled=True),
        lax.all_to_all(key_projection, "head", split_axis=1, concat_axis=0, tiled=True),
        lax.all_to_all(value_projection, "head", split_axis=1, concat_axis=0, tiled=True),
    )
    tokens_dev = q_local.shape[0]
    block_count = tokens_dev // BLOCK_TOKENS
    q_heads = q_local.shape[1] // HEAD_SIZE
    kv_heads = k_local.shape[1] // HEAD_SIZE
    heads_per_group = q_heads // kv_heads
    level_list = partners.shape[1]
    near_count = block_count.bit_length() - 1
    far_count = level_list - near_count
    scaling = 1.0 / math.sqrt(HEAD_SIZE)
    highest = lax.Precision.HIGHEST
    key_value = jnp.stack([k_local, v_local])
    far_sets = [from_behind(key_value, "seq", 2**degree) for degree in range(far_count)]
    block_shape = (2, block_count, BLOCK_TOKENS, kv_heads * HEAD_SIZE)
    own_blocks = key_value.reshape(block_shape)
    near_pool = jnp.concatenate([far_sets[0].reshape(block_shape), own_blocks], axis=1)
    first_block = lax.axis_index("seq") * block_count
    is_valid = partners >= 0
    picked = [own_blocks]
    degree = 0
    target = partners[:, degree] - first_block + block_count
    near_targets = target
    picked.append(jnp.take(near_pool, jnp.clip(target, 0, 2 * block_count - 1), axis=1))
    far_targets = []
    for degree in range(far_count):
        target = partners[:, near_count + degree] - (first_block - 2**degree * block_count)
        far_targets.append(target)
        picked.append(
            jnp.take(
                far_sets[degree].reshape(block_shape), jnp.clip(target, 0, block_count - 1), axis=1
            )
        )
    slot_count_all = 1 + level_list
    key_number = slot_count_all * BLOCK_TOKENS
    gathered = jnp.stack(picked, axis=2).reshape(2, block_count, key_number, kv_heads, HEAD_SIZE)
    row_ids = jnp.arange(BLOCK_TOKENS)[:, None]
    columns = jnp.arange(key_number)[None, :]
    slot_of = columns // BLOCK_TOKENS
    causal = (slot_of == 0) & (columns <= row_ids)
    slot_valid = jnp.concatenate([jnp.ones((block_count, 1), bool), is_valid], axis=1)
    allowed = causal[None] | (slot_of > 0)[None] & slot_valid[:, slot_of[0]][:, None, :]
    query_blocks = q_local.reshape(block_count, BLOCK_TOKENS, q_heads, HEAD_SIZE)
    output_grad_blocks = dout_local.reshape(block_count, BLOCK_TOKENS, q_heads, HEAD_SIZE)
    attn_list = []
    dquery_list = []
    key_row_set = gathered[0, :, :, 0, :]
    value_row_set = gathered[1, :, :, 0, :]
    key_sum = jnp.zeros((block_count, key_number, HEAD_SIZE), jnp.float32)
    value_sum = jnp.zeros((block_count, key_number, HEAD_SIZE), jnp.float32)
    for member in range(heads_per_group):
        query_row_set = query_blocks[:, :, member, :]
        output_grad_rows = output_grad_blocks[:, :, member, :]
        scores = scaling * jnp.einsum(
            "frc,fzc->frz", query_row_set, key_row_set, preferred_element_type=jnp.float32
        )
        scores = jnp.where(allowed, scores, masked_score)
        row_max = jnp.max(scores, axis=-1, keepdims=True)
        exp_scores = jnp.exp(scores - row_max)
        weights = exp_scores / jnp.sum(exp_scores, axis=-1, keepdims=True)
        weights_reduced = weights.astype(jnp.bfloat16)
        attn = jnp.einsum(
            "awv,avq->awq", weights_reduced, value_row_set, preferred_element_type=jnp.float32
        )
        row_dot = jnp.sum(output_grad_rows.astype(jnp.float32) * attn, axis=-1, keepdims=True)
        dweights = jnp.einsum(
            "frc,fzc->frz", output_grad_rows, value_row_set, preferred_element_type=jnp.float32
        )
        score_gradient = (weights * (dweights - row_dot)).astype(jnp.bfloat16)
        dquery = scaling * jnp.einsum(
            "awv,avq->awq", score_gradient, key_row_set, preferred_element_type=jnp.float32
        )
        key_sum = key_sum + scaling * jnp.einsum(
            "ioc,ioa->ica", score_gradient, query_row_set, preferred_element_type=jnp.float32
        )
        value_sum = value_sum + jnp.einsum(
            "ioc,ioa->ica", weights_reduced, output_grad_rows, preferred_element_type=jnp.float32
        )
        attn_list.append(attn)
        dquery_list.append(dquery)
    key_grads = [key_sum]
    value_grads = [value_sum]
    grads = jnp.stack([jnp.stack(key_grads, axis=2), jnp.stack(value_grads, axis=2)])
    grads = grads.reshape(2, block_count, slot_count_all, BLOCK_TOKENS * kv_heads * HEAD_SIZE)
    positions = jnp.arange(2 * block_count)[None, :]
    near_hot = jnp.stack(
        [((near_targets[:, None] == positions) & is_valid[:, 0:1]).astype(jnp.float32)]
    )
    near_sum = jnp.einsum(
        "lqp,sqlx->spx", near_hot, grads[:, :, 1 : 1 + near_count], precision=highest
    )
    own_total = grads[:, :, 0] + near_sum[:, block_count:]
    local_ids = jnp.arange(block_count)[None, :]
    far_parts = []
    for degree in range(far_count):
        column = near_count + degree
        one_hot = (
            (far_targets[degree][:, None] == local_ids) & is_valid[:, column : column + 1]
        ).astype(jnp.float32)
        far_part = jnp.einsum("qp,sqx->spx", one_hot, grads[:, :, 1 + column], precision=highest)
        if degree == 0:
            far_part = far_part + near_sum[:, :block_count]
        far_parts.append(far_part)
    summed = own_total
    for degree in range(far_count):
        summed = summed + from_behind(far_parts[degree], "seq", -(2**degree))
    kv_out = summed.reshape(2, tokens_dev, kv_heads * HEAD_SIZE).astype(jnp.bfloat16)
    attention = (
        jnp.stack(attn_list, axis=2).reshape(tokens_dev, q_heads * HEAD_SIZE).astype(jnp.bfloat16)
    )
    grad_query = (
        jnp.stack(dquery_list, axis=2).reshape(tokens_dev, q_heads * HEAD_SIZE).astype(jnp.bfloat16)
    )
    return (attention, grad_query, kv_out[0], kv_out[1])


def solution(mesh):
    placed = (
        P(("seq", "head"), None),
        P(("seq", "head"), None),
        P(("seq", "head"), None),
        P(("seq", "head"), None),
        P("seq", None),
    )
    return jax.shard_map(
        shards,
        mesh=mesh,
        in_specs=placed,
        out_specs=(P("seq", "head"), P("seq", "head"), P("seq", "head"), P("seq", "head")),
        check_vma=False,
    )
```

profile of v0, /device:TPU:2, one launch (start us, length us, event | category | flops | bytes accessed | tf_op | source)
XLA Modules:
  0.0 144.5 jit_solution(5050257627439415097)
XLA Ops:
  2.1 4.5 %all-to-all-start = ((bf16[32,8,128]{2,0,1:T(8,128)(2,1)}), bf16[32,8,128]{2,0,1:T(8,128)(2,1)S(1)}, u32[]{:S(2)}, u32[]{:S(2)}) async-start(bf16[32,8,128]{2,0,1:T(8,128)(2,1)} %copy_bitcast_fusion.5), calls=%async_computation | async-start | bytes 131072 | tf_op jit(solution)/shard_map/all_to_all | solution.py:25
  7.4 1.7 %fusion.95 = (s32[2]{0:T(128)S(1)}, s32[2]{0:T(128)S(1)}, s32[2]{0:T(128)}, s32[2]{0:T(128)}, s32[2]{0:T(128)}, /*index=5*/s32[2]{0:T(128)}, s32[2]{0:T(128)S(1)...) fusion(s32[2,6]{1,0:T(2,128)} %param.11, s32[]{:T(128)S(6)} %sub.154, ...), kind=kLoop, calls=%fused_computation.221 | loop fusion | flops 32 | bytes 168 | tf_op jit(solution)/shard_map/sub | solution.py:52
  10.7 1.5 %copy_bitcast_fusion.4 = bf16[32,8,128]{2,0,1:T(8,128)(2,1)} fusion(bf16[32,1024]{1,0:T(8,128)(2,1)} %param.9), kind=kLoop, calls=%fused_computation.120 | loop fusion | bytes 131072 | tf_op jit(solution)/shard_map/all_to_all | solution.py:26
  12.9 1.7 %copy.231 = bf16[4,8,8,512]{3,2,0,1:T(8,128)(2,1)} copy(bf16[4,8,8,512]{3,2,1,0:T(8,128)(2,1)} %bitcast.345) | data formatting | bytes 524288 | tf_op jit(solution)/shard_map/all_to_all | solution.py:23
  14.6 2.2 %gather_fusion = pred[896,2]{1,0:T(8,128)(4,1)S(1)} fusion(pred[2,7]{0,1:T(8,128)(4,1)S(1)} %concatenate.9, s32[1024]{0:T(1024)S(1)} %pad_clamp_fusion.6), kind=kCustom, calls=%fused_computation.5 | custom fusion | bytes 7168 | tf_op jit(solution)/shard_map/gather | solution.py:67
  17.0 4.8 %all-to-all-start.1 = ((bf16[32,8,128]{2,0,1:T(8,128)(2,1)}), bf16[32,8,128]{2,0,1:T(8,128)(2,1)S(1)}, u32[]{:S(2)}, u32[]{:S(2)}) async-start(bf16[32,8,128]{2,0,1:T(8,128)(2,1)} %copy_bitcast_fusion.4), calls=%async_computation.1 | async-start | bytes 131072 | tf_op jit(solution)/shard_map/all_to_all | solution.py:26
  21.8 5.6 %all-to-all-done.1 = bf16[32,8,128]{2,0,1:T(8,128)(2,1)S(1)} async-done(((bf16[32,8,128]{2,0,1:T(8,128)(2,1)}), bf16[32,8,128]{2,0,1:T(8,128)(2,1)S(1)}, u32[]{:S(2)}, u32[]{:S(2)}) %all-to-all-start.1) | async-done | bytes 65568 | tf_op jit(solution)/shard_map/all_to_all | solution.py:26
  27.4 3.4 %all-to-all-start.2 = ((bf16[32,8,512]{2,0,1:T(8,128)(2,1)}), bf16[32,8,512]{2,0,1:T(8,128)(2,1)S(1)}, u32[]{:S(2)}, u32[]{:S(2)}) async-start(bf16[32,8,512]{2,0,1:T(8,128)(2,1)} %bitcast.316), calls=%async_computation.2 | async-start | bytes 524288 | tf_op jit(solution)/shard_map/all_to_all | solution.py:23
  30.8 4.0 %collective-permute-start.4 = (bf16[2,256,128]{2,1,0:T(8,128)(2,1)S(1)}, bf16[2,256,128]{2,1,0:T(8,128)(2,1)S(1)}, u32[]{:S(2)}, u32[]{:S(2)}) collective-permute-start(bf16[2,256,128]{2,1,0:T(8,128)(2,1)S(1)} %pad_maximum_fusion.2), channel_id=1, source_target_pairs={{0,128},{8,136},{16,144},{24,152},{32,160},{40,168},{48,176},{56,1... | collective-permute-start | bytes 393224 | tf_op jit(solution)/shard_map/ppermute | solution.py:18
  34.9 1.9 %collective-permute-start.3 = (bf16[2,256,128]{2,1,0:T(8,128)(2,1)S(1)}, bf16[2,256,128]{2,1,0:T(8,128)(2,1)S(1)}, u32[]{:S(2)}, u32[]{:S(2)}) collective-permute-start(bf16[2,256,128]{2,1,0:T(8,128)(2,1)S(1)} %pad_maximum_fusion.2), channel_id=1, source_target_pairs={{0,64},{8,72},{16,80},{24,88},{32,96},{40,104},{48,112},{56,120},{... | collective-permute-start | bytes 393224 | tf_op jit(solution)/shard_map/ppermute | solution.py:18
  36.8 9.1 %collective-permute-start.2 = (bf16[2,256,128]{2,1,0:T(8,128)(2,1)S(1)}, bf16[2,256,128]{2,1,0:T(8,128)(2,1)S(1)}, u32[]{:S(2)}, u32[]{:S(2)}) collective-permute-start(bf16[2,256,128]{2,1,0:T(8,128)(2,1)S(1)} %pad_maximum_fusion.2), channel_id=1, source_target_pairs={{0,32},{8,40},{16,48},{24,56},{32,64},{40,72},{48,80},{56,88},{64,... | collective-permute-start | bytes 393224 | tf_op jit(solution)/shard_map/ppermute | solution.py:18
  45.9 3.4 %collective-permute-start.1 = (bf16[2,256,128]{2,1,0:T(8,128)(2,1)S(1)}, bf16[2,256,128]{2,1,0:T(8,128)(2,1)S(1)}, u32[]{:S(2)}, u32[]{:S(2)}) collective-permute-start(bf16[2,256,128]{2,1,0:T(8,128)(2,1)S(1)} %pad_maximum_fusion.2), channel_id=1, source_target_pairs={{0,16},{8,24},{16,32},{24,40},{32,48},{40,56},{48,64},{56,72},{64,... | collective-permute-start | bytes 393224 | tf_op jit(solution)/shard_map/ppermute | solution.py:18
  49.3 2.9 %collective-permute-start = (bf16[2,256,128]{2,1,0:T(8,128)(2,1)S(1)}, bf16[2,256,128]{2,1,0:T(8,128)(2,1)S(1)}, u32[]{:S(2)}, u32[]{:S(2)}) collective-permute-start(bf16[2,256,128]{2,1,0:T(8,128)(2,1)S(1)} %pad_maximum_fusion.2), channel_id=1, source_target_pairs={{0,8},{8,16},{16,24},{24,32},{32,40},{40,48},{48,56},{56,64},{64,7... | collective-permute-start | bytes 393224 | tf_op jit(solution)/shard_map/ppermute | solution.py:18
  55.0 4.6 %collective-permute-done.1 = bf16[2,256,128]{2,1,0:T(8,128)(2,1)S(1)} collective-permute-done((bf16[2,256,128]{2,1,0:T(8,128)(2,1)S(1)}, bf16[2,256,128]{2,1,0:T(8,128)(2,1)S(1)}, u32[]{:S(2)}, u32[]{:S(2)}) %collective-permute-start.1) | collective-permute-done | bytes 131104 | tf_op jit(solution)/shard_map/ppermute | solution.py:18
  60.1 1.2 collective-permute-done
  63.2 4.4 %all-to-all-start.3 = ((bf16[32,8,512]{2,0,1:T(8,128)(2,1)}), bf16[32,8,512]{2,0,1:T(8,128)(2,1)S(1)}, u32[]{:S(2)}, u32[]{:S(2)}) async-start(bf16[32,8,512]{2,0,1:T(8,128)(2,1)} %bitcast.315), calls=%async_computation.3 | async-start | bytes 524288 | tf_op jit(solution)/shard_map/all_to_all | solution.py:24
  67.9 7.3 %all-to-all-done.3 = bf16[32,8,512]{2,0,1:T(8,128)(2,1)S(1)} async-done(((bf16[32,8,512]{2,0,1:T(8,128)(2,1)}), bf16[32,8,512]{2,0,1:T(8,128)(2,1)S(1)}, u32[]{:S(2)}, u32[]{:S(2)}) %all-to-all-start.3) | async-done | bytes 262176 | tf_op jit(solution)/shard_map/all_to_all | solution.py:24
  76.2 1.1 fusion.123
  77.2 1.6 %fusion.125 = (f32[2,128]{1,0:T(2,128)S(1)}, f32[2,128,896]{1,2,0:T(8,128)S(1)}) fusion(bf16[2,896,128]{2,1,0:T(8,128)(2,1)S(1)} %bitcast.325, pred[2,896]{1,0:T(4,128)(4,1)S(1)} %copy.119, pred[128,896]{0,1:T(8,128)(4,1)} %fusion.38, bf16[2,128,1,128]{3,2,1,0:T(2,128)(2,1)S(1)} %get-tuple-element.26), kind=kOutput, calls=%fused_computation.251 | convolution fusion | flops 59868032 | bytes 1559296 | tf_op jit(solution)/shard_map/sub | solution.py:84
  78.8 1.6 %fusion.128 = (f32[2,128]{1,0:T(2,128)S(1)}, f32[2,128,896]{1,2,0:T(8,128)S(1)}) fusion(bf16[2,896,128]{2,1,0:T(8,128)(2,1)S(1)} %bitcast.326, pred[2,896]{1,0:T(4,128)(4,1)S(1)} %copy.119, pred[128,896]{0,1:T(8,128)(4,1)} %fusion.38, bf16[2,128,1,128]{3,2,1,0:T(2,128)(2,1)S(1)} %get-tuple-element.23), kind=kOutput, calls=%fused_computation.254 | convolution fusion | flops 59868032 | bytes 1559296 | tf_op jit(solution)/shard_map/sub | solution.py:84
  80.5 1.2 fusion.56
  81.7 1.6 %multiply_reduce_fusion.3 = (f32[2,128]{1,0:T(2,128)}, bf16[2,128,1,128]{1,3,0,2:T(8,128)(2,1)}) fusion(bf16[2,128,1,128]{1,3,0,2:T(8,128)(2,1)S(1)} %copy.182, bf16[2,128,896]{1,2,0:T(8,128)(2,1)S(1)} %fusion.39, bf16[2,896,128]{2,1,0:T(8,128)(2,1)S(1)} %bitcast.317), kind=kOutput, calls=%fused_computation.119 | convolution fusion | flops 58851072 | bytes 1049600 | tf_op jit(solution)/shard_map/awv,avq->awq/dot_general | solution.py:87
  83.4 1.0 multiply_reduce_fusion
  84.4 1.5 %fusion.29 = bf16[2,128,896]{1,2,0:T(8,128)(2,1)S(1)} fusion(bf16[2,896,128]{2,1,0:T(8,128)(2,1)S(1)} %bitcast.319, f32[2,128]{1,0:T(2,128)S(1)} %get-tuple-element.35, f32[2,128,896]{1,2,0:T(8,128)} %copy-done.6, f32[2,128]{1,0:T(2,128)S(1)} %get-tuple-element.43, bf16[2,128,1,128]{1,3,0,2:T(8,128)(2,1)S(1)} %copy.185), kind=kOutput, calls=%fused_computation.60 | convolution fusion | flops 59637760 | bytes 1902592 | tf_op jit(solution)/shard_map/frc,fzc->frz/dot_general | solution.py:91
  85.8 1.0 fusion.34
  86.8 1.4 fusion.126
  88.2 1.3 fusion.41
  89.6 1.0 multiply_reduce_fusion.1
  90.9 1.0 fusion.35
  91.8 2.0 %fusion.127 = (f32[2,128]{1,0:T(2,128)}, f32[2,128,896]{1,2,0:T(8,128)}) fusion(bf16[2,896,128]{2,1,0:T(8,128)(2,1)S(1)} %bitcast.330, pred[2,896]{1,0:T(4,128)(4,1)S(1)} %copy.119, pred[128,896]{0,1:T(8,128)(4,1)S(1)} %copy-done.27, bf16[2,128,1,128]{3,2,1,0:T(2,128)(2,1)S(1)} %copy-done.15), kind=kOutput, calls=%fused_computation.253 | convolution fusion | flops 59868032 | bytes 1559296 | tf_op jit(solution)/shard_map/sub | solution.py:84
  93.8 1.3 fusion.40
  95.1 1.0 multiply_reduce_fusion.2
  96.4 1.0 fusion.36
  99.6 1.2 fusion.13
  100.9 1.4 stack.113
  102.3 1.5 %convolution_add_fusion.2 = f32[2,896,128]{2,1,0:T(8,128)S(1)} fusion(f32[2,896,128]{2,1,0:T(8,128)} %fusion.56, bf16[2,128,896]{1,2,0:T(8,128)(2,1)S(1)} %fusion.40, bf16[2,128,1,128]{1,3,0,2:T(8,128)(2,1)S(1)} %copy-done.10), kind=kOutput, calls=%fused_computation.32 | convolution fusion | flops 58949632 | bytes 2359296 | tf_op jit(solution)/shard_map/ioc,ioa->ica/dot_general | solution.py:101
  104.1 1.2 convolution_add_fusion
  105.3 1.4 stack.114
  109.0 3.7 %collective-permute-start.6 = (f32[2,2,16384]{2,1,0:T(2,128)S(1)}, f32[2,2,16384]{2,1,0:T(2,128)S(1)}, u32[]{:S(2)}, u32[]{:S(2)}) collective-permute-start(f32[2,2,16384]{2,1,0:T(2,128)S(1)} %convolution_bitcast_fusion.4), channel_id=1, source_target_pairs={{16,0},{24,8},{32,16},{40,24},{48,32},{56,40},{64,48},{72,56},{80,... | collective-permute-start | bytes 786440 | tf_op jit(solution)/shard_map/ppermute | solution.py:18
  113.3 6.5 %collective-permute-start.7 = (f32[2,2,16384]{2,1,0:T(2,128)S(1)}, f32[2,2,16384]{2,1,0:T(2,128)S(1)}, u32[]{:S(2)}, u32[]{:S(2)}) collective-permute-start(f32[2,2,16384]{2,1,0:T(2,128)S(1)} %convolution_bitcast_fusion.3), channel_id=1, source_target_pairs={{32,0},{40,8},{48,16},{56,24},{64,32},{72,40},{80,48},{88,56},{96,... | collective-permute-start | bytes 786440 | tf_op jit(solution)/shard_map/ppermute | solution.py:18
  119.9 1.3 convolution_bitcast_fusion.2
  121.2 1.9 %collective-permute-start.8 = (f32[2,2,16384]{2,1,0:T(2,128)}, f32[2,2,16384]{2,1,0:T(2,128)S(1)}, u32[]{:S(2)}, u32[]{:S(2)}) collective-permute-start(f32[2,2,16384]{2,1,0:T(2,128)} %convolution_bitcast_fusion.2), channel_id=1, source_target_pairs={{64,0},{72,8},{80,16},{88,24},{96,32},{104,40},{112,48},{120,56},{... | collective-permute-start | bytes 786440 | tf_op jit(solution)/shard_map/ppermute | solution.py:18
  123.2 1.3 convolution_bitcast_fusion.1
  124.5 1.3 collective-permute-start.9
  127.2 1.9 %collective-permute-start.5 = (f32[2,2,16384]{2,1,0:T(2,128)S(1)}, f32[2,2,16384]{2,1,0:T(2,128)S(1)}, u32[]{:S(2)}, u32[]{:S(2)}) collective-permute-start(f32[2,2,16384]{2,1,0:T(2,128)S(1)} %fusion.4), channel_id=1, source_target_pairs={{8,0},{16,8},{24,16},{32,24},{40,32},{48,40},{56,48},{64,56},{72,6... | collective-permute-start | bytes 786440 | tf_op jit(solution)/shard_map/ppermute | solution.py:18
  131.6 4.5 %collective-permute-done.8 = f32[2,2,16384]{2,1,0:T(2,128)S(1)} collective-permute-done((f32[2,2,16384]{2,1,0:T(2,128)}, f32[2,2,16384]{2,1,0:T(2,128)S(1)}, u32[]{:S(2)}, u32[]{:S(2)}) %collective-permute-start.8) | collective-permute-done | bytes 262176 | tf_op jit(solution)/shard_map/ppermute | solution.py:18
  136.1 5.6 %collective-permute-done.5 = f32[2,2,16384]{2,1,0:T(2,128)S(1)} collective-permute-done((f32[2,2,16384]{2,1,0:T(2,128)S(1)}, f32[2,2,16384]{2,1,0:T(2,128)S(1)}, u32[]{:S(2)}, u32[]{:S(2)}) %collective-permute-start.5) | collective-permute-done | bytes 262176 | tf_op jit(solution)/shard_map/ppermute | solution.py:18
  141.6 1.4 fusion.48
  (169 shorter events, 22.1 us)
Async XLA Ops:
  1.5 51.0 %copy-start.19 = (bf16[32,4096]{1,0:T(8,128)(2,1)S(1)}, bf16[32,4096]{1,0:T(8,128)(2,1)}, u32[]{:S(2)}) copy-start(bf16[32,4096]{1,0:T(8,128)(2,1)} %param.10) | copy-start | bytes 786436
  2.1 14.8 %all-to-all-start = ((bf16[32,8,128]{2,0,1:T(8,128)(2,1)}), bf16[32,8,128]{2,0,1:T(8,128)(2,1)S(1)}, u32[]{:S(2)}, u32[]{:S(2)}) async-start(bf16[32,8,128]{2,0,1:T(8,128)(2,1)} %copy_bitcast_fusion.5), calls=%async_computation | async-start | bytes 131072 | tf_op jit(solution)/shard_map/all_to_all | solution.py:25
  17.0 10.4 %all-to-all-start.1 = ((bf16[32,8,128]{2,0,1:T(8,128)(2,1)}), bf16[32,8,128]{2,0,1:T(8,128)(2,1)S(1)}, u32[]{:S(2)}, u32[]{:S(2)}) async-start(bf16[32,8,128]{2,0,1:T(8,128)(2,1)} %copy_bitcast_fusion.4), calls=%async_computation.1 | async-start | bytes 131072 | tf_op jit(solution)/shard_map/all_to_all | solution.py:26
  27.4 35.8 %all-to-all-start.2 = ((bf16[32,8,512]{2,0,1:T(8,128)(2,1)}), bf16[32,8,512]{2,0,1:T(8,128)(2,1)S(1)}, u32[]{:S(2)}, u32[]{:S(2)}) async-start(bf16[32,8,512]{2,0,1:T(8,128)(2,1)} %bitcast.316), calls=%async_computation.2 | async-start | bytes 524288 | tf_op jit(solution)/shard_map/all_to_all | solution.py:23
  30.8 22.4 %collective-permute-start.4 = (bf16[2,256,128]{2,1,0:T(8,128)(2,1)S(1)}, bf16[2,256,128]{2,1,0:T(8,128)(2,1)S(1)}, u32[]{:S(2)}, u32[]{:S(2)}) collective-permute-start(bf16[2,256,128]{2,1,0:T(8,128)(2,1)S(1)} %pad_maximum_fusion.2), channel_id=1, source_target_pairs={{0,128},{8,136},{16,144},{24,152},{32,160},{40,168},{48,176},{56,1... | collective-permute-start | bytes 393224 | tf_op jit(solution)/shard_map/ppermute | solution.py:18
  34.9 18.9 %collective-permute-start.3 = (bf16[2,256,128]{2,1,0:T(8,128)(2,1)S(1)}, bf16[2,256,128]{2,1,0:T(8,128)(2,1)S(1)}, u32[]{:S(2)}, u32[]{:S(2)}) collective-permute-start(bf16[2,256,128]{2,1,0:T(8,128)(2,1)S(1)} %pad_maximum_fusion.2), channel_id=1, source_target_pairs={{0,64},{8,72},{16,80},{24,88},{32,96},{40,104},{48,112},{56,120},{... | collective-permute-start | bytes 393224 | tf_op jit(solution)/shard_map/ppermute | solution.py:18
  36.8 17.6 %collective-permute-start.2 = (bf16[2,256,128]{2,1,0:T(8,128)(2,1)S(1)}, bf16[2,256,128]{2,1,0:T(8,128)(2,1)S(1)}, u32[]{:S(2)}, u32[]{:S(2)}) collective-permute-start(bf16[2,256,128]{2,1,0:T(8,128)(2,1)S(1)} %pad_maximum_fusion.2), channel_id=1, source_target_pairs={{0,32},{8,40},{16,48},{24,56},{32,64},{40,72},{48,80},{56,88},{64,... | collective-permute-start | bytes 393224 | tf_op jit(solution)/shard_map/ppermute | solution.py:18
  45.9 13.6 %collective-permute-start.1 = (bf16[2,256,128]{2,1,0:T(8,128)(2,1)S(1)}, bf16[2,256,128]{2,1,0:T(8,128)(2,1)S(1)}, u32[]{:S(2)}, u32[]{:S(2)}) collective-permute-start(bf16[2,256,128]{2,1,0:T(8,128)(2,1)S(1)} %pad_maximum_fusion.2), channel_id=1, source_target_pairs={{0,16},{8,24},{16,32},{24,40},{32,48},{40,56},{48,64},{56,72},{64,... | collective-permute-start | bytes 393224 | tf_op jit(solution)/shard_map/ppermute | solution.py:18
  49.3 12.0 %collective-permute-start = (bf16[2,256,128]{2,1,0:T(8,128)(2,1)S(1)}, bf16[2,256,128]{2,1,0:T(8,128)(2,1)S(1)}, u32[]{:S(2)}, u32[]{:S(2)}) collective-permute-start(bf16[2,256,128]{2,1,0:T(8,128)(2,1)S(1)} %pad_maximum_fusion.2), channel_id=1, source_target_pairs={{0,8},{8,16},{16,24},{24,32},{32,40},{40,48},{48,56},{56,64},{64,7... | collective-permute-start | bytes 393224 | tf_op jit(solution)/shard_map/ppermute | solution.py:18
  63.2 12.0 %all-to-all-start.3 = ((bf16[32,8,512]{2,0,1:T(8,128)(2,1)}), bf16[32,8,512]{2,0,1:T(8,128)(2,1)S(1)}, u32[]{:S(2)}, u32[]{:S(2)}) async-start(bf16[32,8,512]{2,0,1:T(8,128)(2,1)} %bitcast.315), calls=%async_computation.3 | async-start | bytes 524288 | tf_op jit(solution)/shard_map/all_to_all | solution.py:24
  76.0 20.1 %copy-start.9 = (bf16[2,128,1,128]{1,3,0,2:T(8,128)(2,1)}, bf16[2,128,1,128]{1,3,0,2:T(8,128)(2,1)S(1)}, u32[]{:S(2)}) copy-start(bf16[2,128,1,128]{1,3,0,2:T(8,128)(2,1)S(1)} %copy.183) | copy-start | bytes 196612
  77.2 3.2 %copy-start.11 = (bf16[2,128,1,128]{3,2,1,0:T(2,128)(2,1)}, bf16[2,128,1,128]{3,2,1,0:T(2,128)(2,1)S(1)}, u32[]{:S(2)}) copy-start(bf16[2,128,1,128]{3,2,1,0:T(2,128)(2,1)S(1)} %get-tuple-element.26) | copy-start | bytes 196612
  77.2 3.2 %copy-start.17 = (bf16[2,128,1,128]{3,2,1,0:T(2,128)(2,1)}, bf16[2,128,1,128]{3,2,1,0:T(2,128)(2,1)S(1)}, u32[]{:S(2)}) copy-start(bf16[2,128,1,128]{3,2,1,0:T(2,128)(2,1)S(1)} %get-tuple-element.23) | copy-start | bytes 196612
  77.2 9.6 %copy-start.13 = (bf16[2,128,1,128]{3,2,1,0:T(2,128)(2,1)}, bf16[2,128,1,128]{3,2,1,0:T(2,128)(2,1)S(1)}, u32[]{:S(2)}) copy-start(bf16[2,128,1,128]{3,2,1,0:T(2,128)(2,1)S(1)} %get-tuple-element.24) | copy-start | bytes 196612
  78.8 5.5 %copy-start.6 = (f32[2,128,896]{1,2,0:T(8,128)}, f32[2,128,896]{1,2,0:T(8,128)S(1)}, u32[]{:S(2)}) copy-start(f32[2,128,896]{1,2,0:T(8,128)S(1)} %get-tuple-element.44) | copy-start | bytes 2752516
  80.4 2.9 %copy-start.4 = (f32[2,128,896]{1,2,0:T(8,128)}, f32[2,128,896]{1,2,0:T(8,128)S(1)}, u32[]{:S(2)}) copy-start(f32[2,128,896]{1,2,0:T(8,128)S(1)} %get-tuple-element.50) | copy-start | bytes 2752516
  80.4 2.9 %copy-start.37 = (f32[2,128]{1,0:T(2,128)}, f32[2,128]{1,0:T(2,128)S(1)}, u32[]{:S(2)}) copy-start(f32[2,128]{1,0:T(2,128)S(1)} %get-tuple-element.49) | copy-start | bytes 3076
  84.4 2.5 %copy-start.27 = (pred[128,896]{0,1:T(8,128)(4,1)S(1)}, pred[128,896]{0,1:T(8,128)(4,1)}, u32[]{:S(2)}) copy-start(pred[128,896]{0,1:T(8,128)(4,1)} %fusion.38) | copy-start | bytes 344068
  88.2 2.3 %copy-start.8 = (f32[2,128,896]{1,2,0:T(8,128)S(1)}, f32[2,128,896]{1,2,0:T(8,128)}, u32[]{:S(2)}) copy-start(f32[2,128,896]{1,2,0:T(8,128)} %get-tuple-element.46) | copy-start | bytes 2752516
  93.8 2.3 %copy-start.7 = (f32[2,128,896]{1,2,0:T(8,128)S(1)}, f32[2,128,896]{1,2,0:T(8,128)}, u32[]{:S(2)}) copy-start(f32[2,128,896]{1,2,0:T(8,128)} %get-tuple-element.48) | copy-start | bytes 2752516
  93.8 2.3 %copy-start.40 = (f32[2,128]{1,0:T(2,128)S(1)}, f32[2,128]{1,0:T(2,128)}, u32[]{:S(2)}) copy-start(f32[2,128]{1,0:T(2,128)} %get-tuple-element.47) | copy-start | bytes 3076
  96.1 1.3 copy-start.5
  96.1 1.3 copy-start.38
  96.1 1.3 copy-start.39
  99.6 2.7 %copy-start.10 = (bf16[2,128,1,128]{1,3,0,2:T(8,128)(2,1)S(1)}, bf16[2,128,1,128]{1,3,0,2:T(8,128)(2,1)}, u32[]{:S(2)}) copy-start(bf16[2,128,1,128]{1,3,0,2:T(8,128)(2,1)} %copy-done.9) | copy-start | bytes 196612
  106.7 1.6 %copy-start.32 = (s32[2]{0:T(128)S(1)}, s32[2]{0:T(128)}, u32[]{:S(2)}) copy-start(s32[2]{0:T(128)} %get-tuple-element.10) | copy-start | bytes 28
  106.7 1.6 %copy-start.36 = (pred[2]{0:T(512)(128)(4,1)S(1)}, pred[2]{0:T(512)(128)(4,1)}, u32[]{:S(2)}) copy-start(pred[2]{0:T(512)(128)(4,1)} %get-tuple-element.41) | copy-start | bytes 10
  106.7 5.9 %copy-start.31 = (s32[2]{0:T(128)S(1)}, s32[2]{0:T(128)}, u32[]{:S(2)}) copy-start(s32[2]{0:T(128)} %get-tuple-element.9) | copy-start | bytes 28
  106.7 5.9 %copy-start.35 = (pred[2]{0:T(512)(128)(4,1)S(1)}, pred[2]{0:T(512)(128)(4,1)}, u32[]{:S(2)}) copy-start(pred[2]{0:T(512)(128)(4,1)} %get-tuple-element.40) | copy-start | bytes 10
  107.4 12.4 %copy-start.30 = (s32[2]{0:T(128)S(1)}, s32[2]{0:T(128)}, u32[]{:S(2)}) copy-start(s32[2]{0:T(128)} %get-tuple-element.8) | copy-start | bytes 28
  107.5 12.4 %copy-start.34 = (pred[2]{0:T(512)(128)(4,1)S(1)}, pred[2]{0:T(512)(128)(4,1)}, u32[]{:S(2)}) copy-start(pred[2]{0:T(512)(128)(4,1)} %get-tuple-element.39) | copy-start | bytes 10
  107.5 15.7 %copy-start.29 = (s32[2]{0:T(128)S(1)}, s32[2]{0:T(128)}, u32[]{:S(2)}) copy-start(s32[2]{0:T(128)} %get-tuple-element.7) | copy-start | bytes 28
  107.5 15.7 %copy-start.33 = (pred[2]{0:T(512)(128)(4,1)S(1)}, pred[2]{0:T(512)(128)(4,1)}, u32[]{:S(2)}) copy-start(pred[2]{0:T(512)(128)(4,1)} %get-tuple-element.38) | copy-start | bytes 10
  107.5 18.3 %copy-start.28 = (pred[2]{0:T(512)(128)(4,1)S(1)}, pred[2]{0:T(512)(128)(4,1)}, u32[]{:S(2)}) copy-start(pred[2]{0:T(512)(128)(4,1)} %get-tuple-element.42) | copy-start | bytes 10
  108.3 19.0 %copy-start.1 = (f32[2,2,7,16384]{3,1,0,2:T(2,128)}, f32[2,2,7,16384]{3,1,0,2:T(2,128)S(1)}, u32[]{:S(2)}) copy-start(f32[2,2,7,16384]{3,1,0,2:T(2,128)S(1)} %copy_dynamic-update-slice_fusion) | copy-start | bytes 5505028
  108.9 20.2 %copy-start.3 = (bf16[2,128,896]{1,2,0:T(8,128)(2,1)S(1)}, bf16[2,128,896]{1,2,0:T(8,128)(2,1)}, u32[]{:S(2)}) copy-start(bf16[2,128,896]{1,2,0:T(8,128)(2,1)} %copy-done.2) | copy-start | bytes 1376260
  109.0 22.6 %collective-permute-start.6 = (f32[2,2,16384]{2,1,0:T(2,128)S(1)}, f32[2,2,16384]{2,1,0:T(2,128)S(1)}, u32[]{:S(2)}, u32[]{:S(2)}) collective-permute-start(f32[2,2,16384]{2,1,0:T(2,128)S(1)} %convolution_bitcast_fusion.4), channel_id=1, source_target_pairs={{16,0},{24,8},{32,16},{40,24},{48,32},{56,40},{64,48},{72,56},{80,... | collective-permute-start | bytes 786440 | tf_op jit(solution)/shard_map/ppermute | solution.py:18
  113.3 18.3 %collective-permute-start.7 = (f32[2,2,16384]{2,1,0:T(2,128)S(1)}, f32[2,2,16384]{2,1,0:T(2,128)S(1)}, u32[]{:S(2)}, u32[]{:S(2)}) collective-permute-start(f32[2,2,16384]{2,1,0:T(2,128)S(1)} %convolution_bitcast_fusion.3), channel_id=1, source_target_pairs={{32,0},{40,8},{48,16},{56,24},{64,32},{72,40},{80,48},{88,56},{96,... | collective-permute-start | bytes 786440 | tf_op jit(solution)/shard_map/ppermute | solution.py:18
  119.9 9.7 %copy-start.24 = (bf16[2,128,1,128]{3,1,0,2:T(8,128)(2,1)S(1)}, bf16[2,128,1,128]{3,1,0,2:T(8,128)(2,1)}, u32[]{:S(2)}) copy-start(bf16[2,128,1,128]{3,1,0,2:T(8,128)(2,1)} %fusion.34) | copy-start | bytes 196612
  119.9 9.7 %copy-start.25 = (bf16[2,128,1,128]{3,1,0,2:T(8,128)(2,1)S(1)}, bf16[2,128,1,128]{3,1,0,2:T(8,128)(2,1)}, u32[]{:S(2)}) copy-start(bf16[2,128,1,128]{3,1,0,2:T(8,128)(2,1)} %fusion.35) | copy-start | bytes 196612
  119.9 9.7 %copy-start.26 = (bf16[2,128,1,128]{3,1,0,2:T(8,128)(2,1)S(1)}, bf16[2,128,1,128]{3,1,0,2:T(8,128)(2,1)}, u32[]{:S(2)}) copy-start(bf16[2,128,1,128]{3,1,0,2:T(8,128)(2,1)} %fusion.36) | copy-start | bytes 196612
  121.2 14.8 %collective-permute-start.8 = (f32[2,2,16384]{2,1,0:T(2,128)}, f32[2,2,16384]{2,1,0:T(2,128)S(1)}, u32[]{:S(2)}, u32[]{:S(2)}) collective-permute-start(f32[2,2,16384]{2,1,0:T(2,128)} %convolution_bitcast_fusion.2), channel_id=1, source_target_pairs={{64,0},{72,8},{80,16},{88,24},{96,32},{104,40},{112,48},{120,56},{... | collective-permute-start | bytes 786440 | tf_op jit(solution)/shard_map/ppermute | solution.py:18
  124.5 11.5 %collective-permute-start.9 = (f32[2,2,16384]{2,1,0:T(2,128)}, f32[2,2,16384]{2,1,0:T(2,128)S(1)}, u32[]{:S(2)}, u32[]{:S(2)}) collective-permute-start(f32[2,2,16384]{2,1,0:T(2,128)} %convolution_bitcast_fusion.1), channel_id=1, source_target_pairs={{128,0},{136,8},{144,16},{152,24},{160,32},{168,40},{176,48},{184,... | collective-permute-start | bytes 786440 | tf_op jit(solution)/shard_map/ppermute | solution.py:18
  126.5 4.0 %copy-start.20 = (bf16[2,128,1,128]{1,3,0,2:T(8,128)(2,1)S(1)}, bf16[2,128,1,128]{1,3,0,2:T(8,128)(2,1)}, u32[]{:S(2)}) copy-start(bf16[2,128,1,128]{1,3,0,2:T(8,128)(2,1)} %get-tuple-element.30) | copy-start | bytes 196612
  126.5 4.0 %copy-start.21 = (bf16[2,128,1,128]{1,3,0,2:T(8,128)(2,1)S(1)}, bf16[2,128,1,128]{1,3,0,2:T(8,128)(2,1)}, u32[]{:S(2)}) copy-start(bf16[2,128,1,128]{1,3,0,2:T(8,128)(2,1)} %get-tuple-element.36) | copy-start | bytes 196612
  126.5 4.0 %copy-start.22 = (bf16[2,128,1,128]{1,3,0,2:T(8,128)(2,1)S(1)}, bf16[2,128,1,128]{1,3,0,2:T(8,128)(2,1)}, u32[]{:S(2)}) copy-start(bf16[2,128,1,128]{1,3,0,2:T(8,128)(2,1)} %get-tuple-element.34) | copy-start | bytes 196612
  126.6 4.0 %copy-start.23 = (bf16[2,128,1,128]{1,3,0,2:T(8,128)(2,1)S(1)}, bf16[2,128,1,128]{1,3,0,2:T(8,128)(2,1)}, u32[]{:S(2)}) copy-start(bf16[2,128,1,128]{1,3,0,2:T(8,128)(2,1)} %get-tuple-element.32) | copy-start | bytes 196612
  127.2 14.4 %collective-permute-start.5 = (f32[2,2,16384]{2,1,0:T(2,128)S(1)}, f32[2,2,16384]{2,1,0:T(2,128)S(1)}, u32[]{:S(2)}, u32[]{:S(2)}) collective-permute-start(f32[2,2,16384]{2,1,0:T(2,128)S(1)} %fusion.4), channel_id=1, source_target_pairs={{8,0},{16,8},{24,16},{32,24},{40,32},{48,40},{56,48},{64,56},{72,6... | collective-permute-start | bytes 786440 | tf_op jit(solution)/shard_map/ppermute | solution.py:18
  (7 other events, 7.0 us)
where the time goes:
time: 146 us; the launch traced here: 145 us
  starting transfers between devices  53.8 us (37%)
  waiting for transfers between devices  28.8 us (20%)
  matrix products  28 us (19%)
  local copies, waits for them, and re-layouts  23.6 us (16%)
  other arithmetic  8.61 us (6%)
  between operations  1.62 us (1%)
    ppermute x10, starting transfers between devices, from_behind(): lax.ppermute(value, axis, [(source, source + steps) for source in range(i...  36.7 us
    ppermute x10, waiting for transfers between devices, from_behind(): lax.ppermute(value, axis, [(source, source + steps) for source in range(i...  15.9 us
    all_to_all x1, waiting for transfers between devices, shards(): lax.all_to_all(output_gradient, 'head', split_axis=1, concat_axis=0, tile...  7.33 us
    sub x4, matrix products, shards(): exp_scores = jnp.exp(scores - row_max)  6.54 us
    all_to_all x1, waiting for transfers between devices, shards(): lax.all_to_all(value_projection, 'head', split_axis=1, concat_axis=0, til...  5.61 us
    unnamed x90, local copies, waits for them, and re-layouts  5.56 us
    all_to_all x1, starting transfers between devices, shards(): lax.all_to_all(value_projection, 'head', split_axis=1, concat_axis=0, til...  4.81 us
    dot_general x5, matrix products, shards(): jnp.einsum('qp,sqx->spx', one_hot, grads[:, :, 1 + column], precision=hig...  4.59 us
  transfers between devices with their start and end apart: 14, of which 6 were waited for; matrix products, arithmetic and copies ran while one was open for 16% of the time, Pallas kernels for 0%

commit v1 on v0

v1 whole, which is shorter than its diff:
```python
import functools
import math

import jax
import jax.numpy as jnp
from jax import lax
from jax.experimental import pallas as pl
from jax.experimental.pallas import tpu as pltpu
from jax.sharding import PartitionSpec as P

HEAD_SIZE = 128
BLOCK_TOKENS = 128
MASKED = -1e30
SCALING = 1.0 / math.sqrt(HEAD_SIZE)
VMEM = pl.BlockSpec(memory_space=pltpu.VMEM)
SMEM = pl.BlockSpec(memory_space=pltpu.SMEM)


def ring(value, axis, steps):
    count = lax.axis_size(axis)
    return lax.ppermute(value, axis, [(s, (s + steps) % count) for s in range(count)])


def pack_kernel(first_ref, second_ref, out_ref):
    heads, _, both = out_ref.shape
    width = both // 2
    for head in range(heads):
        columns = slice(head * width, (head + 1) * width)
        out_ref[head, :, :width] = first_ref[:, columns]
        out_ref[head, :, width:] = second_ref[:, columns]


def pack(first, second, heads):
    tokens, columns = first.shape
    return pl.pallas_call(
        pack_kernel,
        out_shape=jax.ShapeDtypeStruct((heads, tokens, 2 * columns // heads), first.dtype),
        in_specs=[VMEM, VMEM],
        out_specs=VMEM,
        compiler_params=pltpu.CompilerParams(vmem_limit_bytes=8 << 20),
    )(first, second)


def dot(a, b, contract):
    return lax.dot_general(a, b, ((contract[:1], contract[1:]), ((), ())), preferred_element_type=jnp.float32)


def main_kernel(far_count, q_heads, partners_ref, qd_ref, kv_ref, *refs):
    far_refs = refs[:far_count]
    own_ref, probs_ref, dscores_ref, cat_ref = refs[far_count : far_count + 4]
    part_refs = refs[far_count + 4 : 2 * far_count + 4]
    (sums_ref,) = refs[2 * far_count + 4 :]
    blocks = kv_ref.shape[0] // BLOCK_TOKENS
    slots = 2 + far_count
    size = BLOCK_TOKENS
    q_columns = q_heads * HEAD_SIZE
    pair = 2

    for b in range(blocks):
        rows = slice(b * size, (b + 1) * size)
        near = kv_ref[(b - 1) * size : b * size, :] if b else far_refs[0][(blocks - 1) * size :, :]
        cat_ref[b, :size, :] = kv_ref[rows, :]
        cat_ref[b, size : 2 * size, :] = near
        for j in range(far_count):
            pick = pl.multiple_of((partners_ref[b, 1 + j] & (blocks - 1)) * size, size)
            cat_ref[b, (2 + j) * size : (3 + j) * size, :] = far_refs[j][pl.ds(pick, size), :]

    causal = lax.broadcasted_iota(jnp.int32, (size, size), 0) <= lax.broadcasted_iota(jnp.int32, (size, size), 1)
    causal = jnp.concatenate([causal] * pair, axis=1)
    for b in range(blocks):
        rows = slice(b * size, (b + 1) * size)
        keys = cat_ref[b, :, :HEAD_SIZE]
        values = cat_ref[b, :, HEAD_SIZE:]
        bias = [jnp.where(partners_ref[b, l] >= 0, 0.0, MASKED).astype(jnp.float32) for l in range(1 + far_count)]
        queries, cotangents = [], []
        for h in range(q_heads):
            queries.append(qd_ref[rows, h * HEAD_SIZE : (h + 1) * HEAD_SIZE])
            cotangents.append(qd_ref[rows, q_columns + h * HEAD_SIZE : q_columns + (h + 1) * HEAD_SIZE])
        for c in range(q_heads // pair):
            columns = slice(c * pair * size, (c + 1) * pair * size)
            query = jnp.concatenate(queries[c * pair : (c + 1) * pair], axis=0)
            cotangent = jnp.concatenate(cotangents[c * pair : (c + 1) * pair], axis=0)
            raw = dot(keys, query, (1, 1))
            scores = [jnp.where(causal, raw[:size], MASKED)]
            scores += [raw[(1 + l) * size : (2 + l) * size] + bias[l] for l in range(1 + far_count)]
            top = functools.reduce(jnp.maximum, scores)
            top = jnp.max(top, axis=0, keepdims=True)
            weights = [jnp.exp((s - top) * SCALING) for s in scores]
            total = jnp.sum(functools.reduce(jnp.add, weights), axis=0, keepdims=True)
            inverse = 1.0 / total
            dprobs = dot(values, cotangent, (1, 1))
            row_dot = jnp.zeros((size, pair * size), jnp.float32)
            for i in range(slots):
                weights[i] = weights[i] * inverse
                low = weights[i].astype(jnp.bfloat16)
                probs_ref[b, i * size : (i + 1) * size, columns] = low
                row_dot = row_dot + low.astype(jnp.float32) * dprobs[i * size : (i + 1) * size]
            row_dot = jnp.sum(row_dot, axis=0, keepdims=True)
            for i in range(slots):
                change = weights[i] * (dprobs[i * size : (i + 1) * size] - row_dot)
                dscores_ref[b, i * size : (i + 1) * size, columns] = change.astype(jnp.bfloat16)
        sums_ref[b, :, :HEAD_SIZE] = SCALING * dot(dscores_ref[b], jnp.concatenate(queries, axis=0), (1, 0))
        sums_ref[b, :, HEAD_SIZE:] = dot(probs_ref[b], jnp.concatenate(cotangents, axis=0), (1, 0))

    for b in range(blocks):
        total = sums_ref[b, :size, :]
        if b + 1 < blocks:
            total = total + sums_ref[b + 1, size : 2 * size, :]
        own_ref[b * size : (b + 1) * size, :] = total
    for j in range(far_count):
        at = slice((2 + j) * size, (3 + j) * size)
        for target in range(blocks):
            total = None
            for b in range(blocks):
                chosen = (partners_ref[b, 1 + j] & (blocks - 1)) == target
                term = jnp.where(chosen, sums_ref[b, at, :], 0.0)
                total = term if total is None else total + term
            if j == 0 and target == blocks - 1:
                total = total + sums_ref[0, size : 2 * size, :]
            part_refs[j][target * size : (target + 1) * size, :] = total.astype(jnp.bfloat16)


def outputs_kernel(q_heads, probs_ref, dscores_ref, cat_ref, attention_ref, grad_query_ref):
    size = BLOCK_TOKENS
    for b in range(probs_ref.shape[0]):
        rows = slice(b * size, (b + 1) * size)
        attention = dot(cat_ref[b, :, HEAD_SIZE:], probs_ref[b], (0, 0))
        grad_query = SCALING * dot(cat_ref[b, :, :HEAD_SIZE], dscores_ref[b], (0, 0))
        for h in range(q_heads):
            columns = slice(h * HEAD_SIZE, (h + 1) * HEAD_SIZE)
            at = slice(h * size, (h + 1) * size)
            attention_ref[rows, columns] = attention[:, at].T.astype(jnp.bfloat16)
            grad_query_ref[rows, columns] = grad_query[:, at].T.astype(jnp.bfloat16)


def sum_kernel(own_ref, *refs):
    key_ref, value_ref = refs[-2:]
    total = own_ref[...]
    for ref in refs[:-2]:
        total = total + ref[...].astype(jnp.float32)
    key_ref[...] = total[:, :HEAD_SIZE].astype(jnp.bfloat16)
    value_ref[...] = total[:, HEAD_SIZE:].astype(jnp.bfloat16)


def shards(query_projection, key_projection, value_projection, output_gradient, partners):
    heads = lax.axis_size("head")
    kv = lax.all_to_all(pack(key_projection, value_projection, heads), "head", 0, 0, tiled=True)
    qd = lax.all_to_all(pack(query_projection, output_gradient, heads), "head", 0, 0, tiled=True)
    kv = kv.reshape(-1, kv.shape[-1])
    qd = qd.reshape(-1, qd.shape[-1])
    tokens = kv.shape[0]
    blocks = tokens // BLOCK_TOKENS
    q_heads = qd.shape[1] // (2 * HEAD_SIZE)
    far_count = partners.shape[1] - 1
    fars = [ring(kv, "seq", 2**j) for j in range(far_count)]
    keys = (2 + far_count) * BLOCK_TOKENS
    big = (blocks, keys, q_heads * BLOCK_TOKENS)
    own, probs, dscores, cat, *parts = pl.pallas_call(
        functools.partial(main_kernel, far_count, q_heads),
        out_shape=[
            jax.ShapeDtypeStruct((tokens, 2 * HEAD_SIZE), jnp.float32),
            jax.ShapeDtypeStruct(big, jnp.bfloat16),
            jax.ShapeDtypeStruct(big, jnp.bfloat16),
            jax.ShapeDtypeStruct((blocks, keys, 2 * HEAD_SIZE), jnp.bfloat16),
        ]
        + [jax.ShapeDtypeStruct((tokens, 2 * HEAD_SIZE), jnp.bfloat16)] * far_count,
        in_specs=[SMEM] + [VMEM] * (2 + far_count),
        out_specs=[VMEM] * (4 + far_count),
        scratch_shapes=[pltpu.VMEM((blocks, keys, 2 * HEAD_SIZE), jnp.float32)],
        compiler_params=pltpu.CompilerParams(vmem_limit_bytes=32 << 20),
    )(partners, qd, kv, *fars)
    received = [ring(part, "seq", -(2**j)) for j, part in enumerate(parts)]
    attention, grad_query = pl.pallas_call(
        functools.partial(outputs_kernel, q_heads),
        out_shape=[jax.ShapeDtypeStruct((tokens, q_heads * HEAD_SIZE), jnp.bfloat16)] * 2,
        in_specs=[VMEM] * 3,
        out_specs=[VMEM] * 2,
        compiler_params=pltpu.CompilerParams(vmem_limit_bytes=32 << 20),
    )(probs, dscores, cat)
    key_gradient, value_gradient = pl.pallas_call(
        sum_kernel,
        out_shape=[jax.ShapeDtypeStruct((tokens, HEAD_SIZE), jnp.bfloat16)] * 2,
        in_specs=[VMEM] * (1 + far_count),
        out_specs=[VMEM] * 2,
        compiler_params=pltpu.CompilerParams(vmem_limit_bytes=8 << 20),
    )(own, *received)
    return (attention, grad_query, key_gradient, value_gradient)


def solution(mesh):
    placed = (
        P(("seq", "head"), None),
        P(("seq", "head"), None),
        P(("seq", "head"), None),
        P(("seq", "head"), None),
        P("seq", None),
    )
    return jax.shard_map(
        shards,
        mesh=mesh,
        in_specs=placed,
        out_specs=(P("seq", "head"), P("seq", "head"), P("seq", "head"), P("seq", "head")),
        check_vma=False,
    )
```

time: 146 us -> 67.1 us (0.46)
  the two profiles are of different devices: /device:TPU:2 before, /device:TPU:40 now
where the time goes in v1:
time: 67.1 us; the launch traced here: 66.7 us
  starting transfers between devices  31.2 us (46%)
  waiting for transfers between devices  22.8 us (34%)
  Pallas kernels  8.43 us (13%)
  local copies, waits for them, and re-layouts  3.57 us (5%)
    ppermute x10, starting transfers between devices, ring(): lax.ppermute(value, axis, [(s, (s + steps) % count) for s in range(count)])  21.5 us
    ppermute x10, waiting for transfers between devices, ring(): lax.ppermute(value, axis, [(s, (s + steps) % count) for s in range(count)])  20.8 us
    all_to_all x1, starting transfers between devices, shards(): lax.all_to_all(pack(key_projection, value_projection, heads), 'head', 0,...  4.92 us
    all_to_all x1, starting transfers between devices, shards(): lax.all_to_all(pack(query_projection, output_gradient, heads), 'head', 0,...  4.86 us
    pallas_call x1, Pallas kernels, shards(): pl.pallas_call(functools.partial(main_kernel, far_count, q_heads), out_sh...  4.52 us
    unnamed x10, local copies, waits for them, and re-layouts  3.57 us
    all_to_all x1, waiting for transfers between devices, shards(): lax.all_to_all(pack(key_projection, value_projection, heads), 'head', 0,...  1.94 us
    pallas_call x1, Pallas kernels, shards(): pl.pallas_call(functools.partial(outputs_kernel, q_heads), out_shape=[jax...  1.65 us
  transfers between devices with their start and end apart: 12, of which 6 were waited for; matrix products, arithmetic and copies ran while one was open for 0% of the time, Pallas kernels for 4%

profile of v1, /device:TPU:40, one launch (start us, length us, event | category | flops | bytes accessed | tf_op | source)
XLA Modules:
  0.0 66.7 jit_solution(1798137245564293310)
XLA Ops:
  0.6 0.0 copy-start.2
  0.6 0.8 %copy-done.2 = bf16[32,1024]{1,0:T(8,128)(2,1)S(1)} copy-done((bf16[32,1024]{1,0:T(8,128)(2,1)S(1)}, bf16[32,1024]{1,0:T(8,128)(2,1)}, u32[]{:S(2)}) %copy-start.2) | copy-done | bytes 65560
  1.5 0.0 copy-start.3
  1.5 0.8 %copy-done.3 = bf16[32,1024]{1,0:T(8,128)(2,1)S(1)} copy-done((bf16[32,1024]{1,0:T(8,128)(2,1)S(1)}, bf16[32,1024]{1,0:T(8,128)(2,1)}, u32[]{:S(2)}) %copy-start.3) | copy-done | bytes 65560
  2.3 0.0 copy-start.4
  2.3 0.7 %shard_map.85 = bf16[8,32,256]{2,1,0:T(8,128)(2,1)} custom-call(bf16[32,1024]{1,0:T(8,128)(2,1)S(1)} %copy-done.2, bf16[32,1024]{1,0:T(8,128)(2,1)S(1)} %copy-done.3), custom_call_target="tpu_custom_call" | custom-call | tf_op jit(solution)/shard_map/pallas_call | solution.py:35
  3.0 4.9 %all-to-all-start.1 = ((bf16[8,32,256]{2,1,0:T(8,128)(2,1)}), bf16[8,32,256]{2,1,0:T(8,128)(2,1)S(1)}, u32[]{:S(2)}, u32[]{:S(2)}) async-start(bf16[8,32,256]{2,1,0:T(8,128)(2,1)} %shard_map.85), calls=%async_computation.1 | async-start | bytes 262144 | tf_op jit(solution)/shard_map/all_to_all | solution.py:147
  7.9 0.0 copy-start
  7.9 0.9 %copy-done = bf16[32,4096]{1,0:T(8,128)(2,1)S(1)} copy-done((bf16[32,4096]{1,0:T(8,128)(2,1)S(1)}, bf16[32,4096]{1,0:T(8,128)(2,1)}, u32[]{:S(2)}) %copy-start) | copy-done | bytes 262168
  8.9 0.0 copy-start.1
  8.9 0.9 %copy-done.1 = bf16[32,4096]{1,0:T(8,128)(2,1)S(1)} copy-done((bf16[32,4096]{1,0:T(8,128)(2,1)S(1)}, bf16[32,4096]{1,0:T(8,128)(2,1)}, u32[]{:S(2)}) %copy-start.1) | copy-done | bytes 262168
  9.8 0.8 %shard_map.84 = bf16[8,32,1024]{2,1,0:T(8,128)(2,1)} custom-call(bf16[32,4096]{1,0:T(8,128)(2,1)S(1)} %copy-done, bf16[32,4096]{1,0:T(8,128)(2,1)S(1)} %copy-done.1), custom_call_target="tpu_custom_call" | custom-call | tf_op jit(solution)/shard_map/pallas_call | solution.py:35
  10.6 1.9 %all-to-all-done.1 = bf16[8,32,256]{2,1,0:T(8,128)(2,1)S(1)} async-done(((bf16[8,32,256]{2,1,0:T(8,128)(2,1)}), bf16[8,32,256]{2,1,0:T(8,128)(2,1)S(1)}, u32[]{:S(2)}, u32[]{:S(2)}) %all-to-all-start.1) | async-done | bytes 131104 | tf_op jit(solution)/shard_map/all_to_all | solution.py:147
  12.6 4.9 %all-to-all-start = ((bf16[8,32,1024]{2,1,0:T(8,128)(2,1)}), bf16[8,32,1024]{2,1,0:T(8,128)(2,1)S(1)}, u32[]{:S(2)}, u32[]{:S(2)}) async-start(bf16[8,32,1024]{2,1,0:T(8,128)(2,1)} %shard_map.84), calls=%async_computation | async-start | bytes 1048576 | tf_op jit(solution)/shard_map/all_to_all | solution.py:148
  17.4 3.0 %collective-permute-start.4 = (bf16[256,256]{1,0:T(8,128)(2,1)S(1)}, bf16[256,256]{1,0:T(8,128)(2,1)S(1)}, u32[]{:S(2)}, u32[]{:S(2)}) collective-permute-start(bf16[256,256]{1,0:T(8,128)(2,1)S(1)} %bitcast.3), channel_id=1, source_target_pairs={{0,128},{8,136},{16,144},{24,152},{32,160},{40,168},{48,176},{56,1... | collective-permute-start | bytes 393224 | tf_op jit(solution)/shard_map/ppermute | solution.py:21
  20.5 0.6 collective-permute-start.3
  21.1 6.3 %collective-permute-start.2 = (bf16[256,256]{1,0:T(8,128)(2,1)S(1)}, bf16[256,256]{1,0:T(8,128)(2,1)S(1)}, u32[]{:S(2)}, u32[]{:S(2)}) collective-permute-start(bf16[256,256]{1,0:T(8,128)(2,1)S(1)} %bitcast.5), channel_id=1, source_target_pairs={{0,32},{8,40},{16,48},{24,56},{32,64},{40,72},{48,80},{56,88},{64,... | collective-permute-start | bytes 393224 | tf_op jit(solution)/shard_map/ppermute | solution.py:21
  27.4 1.5 %collective-permute-start.1 = (bf16[256,256]{1,0:T(8,128)(2,1)S(1)}, bf16[256,256]{1,0:T(8,128)(2,1)S(1)}, u32[]{:S(2)}, u32[]{:S(2)}) collective-permute-start(bf16[256,256]{1,0:T(8,128)(2,1)S(1)} %bitcast.6), channel_id=1, source_target_pairs={{0,16},{8,24},{16,32},{24,40},{32,48},{40,56},{48,64},{56,72},{64,... | collective-permute-start | bytes 393224 | tf_op jit(solution)/shard_map/ppermute | solution.py:21
  28.8 0.0 collective-permute-start
  28.8 0.0 collective-permute-done.4.refs_4_
  28.8 0.0 collective-permute-done.3.refs_3_
  28.8 6.7 %collective-permute-done.2.refs_2_ = bf16[256,256]{1,0:T(8,128)(2,1)S(1)} collective-permute-done((bf16[256,256]{1,0:T(8,128)(2,1)S(1)}, bf16[256,256]{1,0:T(8,128)(2,1)S(1)}, u32[]{:S(2)}, u32[]{:S(2)}) %collective-permute-start.2) | collective-permute-done | bytes 131104 | tf_op jit(solution)/shard_map/ppermute | solution.py:21
  35.5 6.0 %collective-permute-done.1.refs_1_ = bf16[256,256]{1,0:T(8,128)(2,1)S(1)} collective-permute-done((bf16[256,256]{1,0:T(8,128)(2,1)S(1)}, bf16[256,256]{1,0:T(8,128)(2,1)S(1)}, u32[]{:S(2)}, u32[]{:S(2)}) %collective-permute-start.1) | collective-permute-done | bytes 131104 | tf_op jit(solution)/shard_map/ppermute | solution.py:21
  41.6 0.1 collective-permute-done.refs_0_
  41.7 0.0 all-to-all-done
  41.7 0.0 copy-done.4
  41.7 4.5 %shard_map.86 = (f32[256,256]{1,0:T(8,128)S(1)}, bf16[2,896,512]{2,1,0:T(8,128)(2,1)S(1)}, bf16[2,896,512]{2,1,0:T(8,128)(2,1)S(1)}, bf16[2,896,256]{2,1,0:T(8,1...) custom-call(s32[2,6]{1,0:T(2,128)S(1)} %copy-done.4, ...), custom_call_target="tpu_custom_call" | custom-call | tf_op jit(solution)/shard_map/pallas_call | solution.py:158
  46.2 2.8 %collective-permute-start.5 = (bf16[256,256]{1,0:T(8,128)(2,1)S(1)}, bf16[256,256]{1,0:T(8,128)(2,1)S(1)}, u32[]{:S(2)}, u32[]{:S(2)}) collective-permute-start(bf16[256,256]{1,0:T(8,128)(2,1)S(1)} %get-tuple-element.23), channel_id=1, source_target_pairs={{0,248},{8,0},{16,8},{24,16},{32,24},{40,32},{48,40},{56,48},{64,5... | collective-permute-start | bytes 393224 | tf_op jit(solution)/shard_map/ppermute | solution.py:21
  49.0 1.1 %collective-permute-start.6 = (bf16[256,256]{1,0:T(8,128)(2,1)S(1)}, bf16[256,256]{1,0:T(8,128)(2,1)S(1)}, u32[]{:S(2)}, u32[]{:S(2)}) collective-permute-start(bf16[256,256]{1,0:T(8,128)(2,1)S(1)} %get-tuple-element.24), channel_id=1, source_target_pairs={{0,240},{8,248},{16,0},{24,8},{32,16},{40,24},{48,32},{56,40},{64,... | collective-permute-start | bytes 393224 | tf_op jit(solution)/shard_map/ppermute | solution.py:21
  50.2 5.0 %collective-permute-start.7 = (bf16[256,256]{1,0:T(8,128)(2,1)S(1)}, bf16[256,256]{1,0:T(8,128)(2,1)S(1)}, u32[]{:S(2)}, u32[]{:S(2)}) collective-permute-start(bf16[256,256]{1,0:T(8,128)(2,1)S(1)} %get-tuple-element.25), channel_id=1, source_target_pairs={{0,224},{8,232},{16,240},{24,248},{32,0},{40,8},{48,16},{56,24},{6... | collective-permute-start | bytes 393224 | tf_op jit(solution)/shard_map/ppermute | solution.py:21
  55.1 0.6 collective-permute-start.8
  55.7 0.6 collective-permute-start.9
  56.3 1.6 %shard_map.87 = (bf16[256,512]{1,0:T(8,128)(2,1)}, bf16[256,512]{1,0:T(8,128)(2,1)}) custom-call(bf16[2,896,512]{2,1,0:T(8,128)(2,1)S(1)} %get-tuple-element.17.probs_ref, bf16[2,896,512]{2,1,0:T(8,128)(2,1)S(1)} %get-tuple-element.18.dscores_ref, bf16[2,896,256]{2,1,0:T(8,128)(2,1)S(1)} %get-tuple-element.19.cat_ref), custom_call_target="tpu_custom_call" | custom-call | tf_op jit(solution)/shard_map/pallas_call | solution.py:173
  58.0 0.0 collective-permute-done.5.refs_0_
  58.0 3.2 %collective-permute-done.6.refs_1_ = bf16[256,256]{1,0:T(8,128)(2,1)S(1)} collective-permute-done((bf16[256,256]{1,0:T(8,128)(2,1)S(1)}, bf16[256,256]{1,0:T(8,128)(2,1)S(1)}, u32[]{:S(2)}, u32[]{:S(2)}) %collective-permute-start.6) | collective-permute-done | bytes 131104 | tf_op jit(solution)/shard_map/ppermute | solution.py:21
  61.2 4.7 %collective-permute-done.7.refs_2_ = bf16[256,256]{1,0:T(8,128)(2,1)S(1)} collective-permute-done((bf16[256,256]{1,0:T(8,128)(2,1)S(1)}, bf16[256,256]{1,0:T(8,128)(2,1)S(1)}, u32[]{:S(2)}, u32[]{:S(2)}) %collective-permute-start.7) | collective-permute-done | bytes 131104 | tf_op jit(solution)/shard_map/ppermute | solution.py:21
  65.9 0.0 collective-permute-done.8.refs_3_
  65.9 0.0 collective-permute-done.9.refs_4_
  65.9 0.7 %shard_map.88 = (bf16[256,128]{1,0:T(8,128)(2,1)}, bf16[256,128]{1,0:T(8,128)(2,1)}) custom-call(f32[256,256]{1,0:T(8,128)S(1)} %get-tuple-element.22.own_ref, bf16[256,256]{1,0:T(8,128)(2,1)S(1)} %collective-permute-done.5.refs_0_, bf16[256,256]{1,0:T(8,128)(2,1)S(1)} %collective-permute-done.6.refs_1_, ...), custom_call_target="tpu_custom_call" | custom-call | tf_op jit(solution)/shard_map/pallas_call | solution.py:180
Async XLA Ops:
  0.6 0.8 %copy-start.2 = (bf16[32,1024]{1,0:T(8,128)(2,1)S(1)}, bf16[32,1024]{1,0:T(8,128)(2,1)}, u32[]{:S(2)}) copy-start(bf16[32,1024]{1,0:T(8,128)(2,1)} %first_ref.3) | copy-start | bytes 196612
  1.5 0.8 %copy-start.3 = (bf16[32,1024]{1,0:T(8,128)(2,1)S(1)}, bf16[32,1024]{1,0:T(8,128)(2,1)}, u32[]{:S(2)}) copy-start(bf16[32,1024]{1,0:T(8,128)(2,1)} %second_ref.3) | copy-start | bytes 196612
  2.3 39.4 %copy-start.4 = (s32[2,6]{1,0:T(2,128)S(1)}, s32[2,6]{1,0:T(2,128)}, u32[]{:S(2)}) copy-start(s32[2,6]{1,0:T(2,128)} %partners_ref.1) | copy-start | bytes 148
  3.0 9.6 %all-to-all-start.1 = ((bf16[8,32,256]{2,1,0:T(8,128)(2,1)}), bf16[8,32,256]{2,1,0:T(8,128)(2,1)S(1)}, u32[]{:S(2)}, u32[]{:S(2)}) async-start(bf16[8,32,256]{2,1,0:T(8,128)(2,1)} %shard_map.85), calls=%async_computation.1 | async-start | bytes 262144 | tf_op jit(solution)/shard_map/all_to_all | solution.py:147
  7.9 0.9 %copy-start = (bf16[32,4096]{1,0:T(8,128)(2,1)S(1)}, bf16[32,4096]{1,0:T(8,128)(2,1)}, u32[]{:S(2)}) copy-start(bf16[32,4096]{1,0:T(8,128)(2,1)} %first_ref.2) | copy-start | bytes 786436
  8.9 0.9 %copy-start.1 = (bf16[32,4096]{1,0:T(8,128)(2,1)S(1)}, bf16[32,4096]{1,0:T(8,128)(2,1)}, u32[]{:S(2)}) copy-start(bf16[32,4096]{1,0:T(8,128)(2,1)} %second_ref.2) | copy-start | bytes 786436
  12.6 29.1 %all-to-all-start = ((bf16[8,32,1024]{2,1,0:T(8,128)(2,1)}), bf16[8,32,1024]{2,1,0:T(8,128)(2,1)S(1)}, u32[]{:S(2)}, u32[]{:S(2)}) async-start(bf16[8,32,1024]{2,1,0:T(8,128)(2,1)} %shard_map.84), calls=%async_computation | async-start | bytes 1048576 | tf_op jit(solution)/shard_map/all_to_all | solution.py:148
  17.4 11.4 %collective-permute-start.4 = (bf16[256,256]{1,0:T(8,128)(2,1)S(1)}, bf16[256,256]{1,0:T(8,128)(2,1)S(1)}, u32[]{:S(2)}, u32[]{:S(2)}) collective-permute-start(bf16[256,256]{1,0:T(8,128)(2,1)S(1)} %bitcast.3), channel_id=1, source_target_pairs={{0,128},{8,136},{16,144},{24,152},{32,160},{40,168},{48,176},{56,1... | collective-permute-start | bytes 393224 | tf_op jit(solution)/shard_map/ppermute | solution.py:21
  20.5 8.4 %collective-permute-start.3 = (bf16[256,256]{1,0:T(8,128)(2,1)S(1)}, bf16[256,256]{1,0:T(8,128)(2,1)S(1)}, u32[]{:S(2)}, u32[]{:S(2)}) collective-permute-start(bf16[256,256]{1,0:T(8,128)(2,1)S(1)} %bitcast.4), channel_id=1, source_target_pairs={{0,64},{8,72},{16,80},{24,88},{32,96},{40,104},{48,112},{56,120},{... | collective-permute-start | bytes 393224 | tf_op jit(solution)/shard_map/ppermute | solution.py:21
  21.1 14.5 %collective-permute-start.2 = (bf16[256,256]{1,0:T(8,128)(2,1)S(1)}, bf16[256,256]{1,0:T(8,128)(2,1)S(1)}, u32[]{:S(2)}, u32[]{:S(2)}) collective-permute-start(bf16[256,256]{1,0:T(8,128)(2,1)S(1)} %bitcast.5), channel_id=1, source_target_pairs={{0,32},{8,40},{16,48},{24,56},{32,64},{40,72},{48,80},{56,88},{64,... | collective-permute-start | bytes 393224 | tf_op jit(solution)/shard_map/ppermute | solution.py:21
  27.4 14.2 %collective-permute-start.1 = (bf16[256,256]{1,0:T(8,128)(2,1)S(1)}, bf16[256,256]{1,0:T(8,128)(2,1)S(1)}, u32[]{:S(2)}, u32[]{:S(2)}) collective-permute-start(bf16[256,256]{1,0:T(8,128)(2,1)S(1)} %bitcast.6), channel_id=1, source_target_pairs={{0,16},{8,24},{16,32},{24,40},{32,48},{40,56},{48,64},{56,72},{64,... | collective-permute-start | bytes 393224 | tf_op jit(solution)/shard_map/ppermute | solution.py:21
  28.8 12.9 %collective-permute-start = (bf16[256,256]{1,0:T(8,128)(2,1)S(1)}, bf16[256,256]{1,0:T(8,128)(2,1)S(1)}, u32[]{:S(2)}, u32[]{:S(2)}) collective-permute-start(bf16[256,256]{1,0:T(8,128)(2,1)S(1)} %bitcast.7), channel_id=1, source_target_pairs={{0,8},{8,16},{16,24},{24,32},{32,40},{40,48},{48,56},{56,64},{64,7... | collective-permute-start | bytes 393224 | tf_op jit(solution)/shard_map/ppermute | solution.py:21
  46.2 11.7 %collective-permute-start.5 = (bf16[256,256]{1,0:T(8,128)(2,1)S(1)}, bf16[256,256]{1,0:T(8,128)(2,1)S(1)}, u32[]{:S(2)}, u32[]{:S(2)}) collective-permute-start(bf16[256,256]{1,0:T(8,128)(2,1)S(1)} %get-tuple-element.23), channel_id=1, source_target_pairs={{0,248},{8,0},{16,8},{24,16},{32,24},{40,32},{48,40},{56,48},{64,5... | collective-permute-start | bytes 393224 | tf_op jit(solution)/shard_map/ppermute | solution.py:21
  49.0 12.2 %collective-permute-start.6 = (bf16[256,256]{1,0:T(8,128)(2,1)S(1)}, bf16[256,256]{1,0:T(8,128)(2,1)S(1)}, u32[]{:S(2)}, u32[]{:S(2)}) collective-permute-start(bf16[256,256]{1,0:T(8,128)(2,1)S(1)} %get-tuple-element.24), channel_id=1, source_target_pairs={{0,240},{8,248},{16,0},{24,8},{32,16},{40,24},{48,32},{56,40},{64,... | collective-permute-start | bytes 393224 | tf_op jit(solution)/shard_map/ppermute | solution.py:21
  50.2 15.8 %collective-permute-start.7 = (bf16[256,256]{1,0:T(8,128)(2,1)S(1)}, bf16[256,256]{1,0:T(8,128)(2,1)S(1)}, u32[]{:S(2)}, u32[]{:S(2)}) collective-permute-start(bf16[256,256]{1,0:T(8,128)(2,1)S(1)} %get-tuple-element.25), channel_id=1, source_target_pairs={{0,224},{8,232},{16,240},{24,248},{32,0},{40,8},{48,16},{56,24},{6... | collective-permute-start | bytes 393224 | tf_op jit(solution)/shard_map/ppermute | solution.py:21
  55.1 10.8 %collective-permute-start.8 = (bf16[256,256]{1,0:T(8,128)(2,1)S(1)}, bf16[256,256]{1,0:T(8,128)(2,1)S(1)}, u32[]{:S(2)}, u32[]{:S(2)}) collective-permute-start(bf16[256,256]{1,0:T(8,128)(2,1)S(1)} %get-tuple-element.26), channel_id=1, source_target_pairs={{0,192},{8,200},{16,208},{24,216},{32,224},{40,232},{48,240},{56,2... | collective-permute-start | bytes 393224 | tf_op jit(solution)/shard_map/ppermute | solution.py:21
  55.7 10.2 %collective-permute-start.9 = (bf16[256,256]{1,0:T(8,128)(2,1)S(1)}, bf16[256,256]{1,0:T(8,128)(2,1)S(1)}, u32[]{:S(2)}, u32[]{:S(2)}) collective-permute-start(bf16[256,256]{1,0:T(8,128)(2,1)S(1)} %get-tuple-element.27), channel_id=1, source_target_pairs={{0,128},{8,136},{16,144},{24,152},{32,160},{40,168},{48,176},{56,1... | collective-permute-start | bytes 393224 | tf_op jit(solution)/shard_map/ppermute | solution.py:21

commit v2 on v1

--- a/solution.py
+++ b/solution.py
@@ -14,6 +14,8 @@
 SCALING = 1.0 / math.sqrt(HEAD_SIZE)
 VMEM = pl.BlockSpec(memory_space=pltpu.VMEM)
 SMEM = pl.BlockSpec(memory_space=pltpu.SMEM)
+HBM = pl.BlockSpec(memory_space=pltpu.HBM)
+EARLY = (2, 0)
 
 
 def ring(value, axis, steps):
@@ -21,49 +23,75 @@
     return lax.ppermute(value, axis, [(s, (s + steps) % count) for s in range(count)])
 
 
-def pack_kernel(first_ref, second_ref, out_ref):
-    heads, _, both = out_ref.shape
-    width = both // 2
-    for head in range(heads):
-        columns = slice(head * width, (head + 1) * width)
-        out_ref[head, :, :width] = first_ref[:, columns]
-        out_ref[head, :, width:] = second_ref[:, columns]
-
-
-def pack(first, second, heads):
-    tokens, columns = first.shape
+def pack_kernel(*refs):
+    sources, packed, sems = refs[:4], refs[4:6], refs[6]
+    heads = packed[0].shape[0]
+    copies = []
+    for i, source in enumerate(sources):
+        target = packed[i // 2]
+        width = source.shape[1] // heads
+        for head in range(heads):
+            copies.append(
+                pltpu.make_async_copy(
+                    source.at[:, pl.ds(head * width, width)],
+                    target.at[head, :, pl.ds((i % 2) * width, width)],
+                    sems.at[i, head],
+                )
+            )
+    for copy in copies:
+        copy.start()
+    for copy in copies:
+        copy.wait()
+
+
+def pack(arrays, heads):
+    def packed(array):
+        return jax.ShapeDtypeStruct((heads, array.shape[0], 2 * array.shape[1] // heads), array.dtype)
+
     return pl.pallas_call(
         pack_kernel,
-        out_shape=jax.ShapeDtypeStruct((heads, tokens, 2 * columns // heads), first.dtype),
-        in_specs=[VMEM, VMEM],
-        out_specs=VMEM,
-        compiler_params=pltpu.CompilerParams(vmem_limit_bytes=8 << 20),
-    )(first, second)
+        out_shape=[packed(arrays[0]), packed(arrays[2])],
+        in_specs=[HBM] * 4,
+        out_specs=[VMEM] * 2,
+        scratch_shapes=[pltpu.SemaphoreType.DMA((4, heads))],
+        compiler_params=pltpu.CompilerParams(vmem_limit_bytes=60 << 20),
+    )(*arrays)
 
 
 def dot(a, b, contract):
     return lax.dot_general(a, b, ((contract[:1], contract[1:]), ((), ())), preferred_element_type=jnp.float32)
 
 
-def main_kernel(far_count, q_heads, partners_ref, qd_ref, kv_ref, *refs):
-    far_refs = refs[:far_count]
-    own_ref, probs_ref, dscores_ref, cat_ref = refs[far_count : far_count + 4]
-    part_refs = refs[far_count + 4 : 2 * far_count + 4]
-    (sums_ref,) = refs[2 * far_count + 4 :]
-    blocks = kv_ref.shape[0] // BLOCK_TOKENS
+def fill(cat_ref, partners_ref, fars, kv_ref=None):
+    blocks = cat_ref.shape[0]
+    size = BLOCK_TOKENS
+    for b in range(blocks):
+        if kv_ref is not None:
+            cat_ref[b, :size, :] = kv_ref[b * size : (b + 1) * size, :]
+            if b:
+                cat_ref[b, size : 2 * size, :] = kv_ref[(b - 1) * size : b * size, :]
+        for j, far_ref in fars.items():
+            if b == 0 and j == 0:
+                cat_ref[b, size : 2 * size, :] = far_ref[(blocks - 1) * size :, :]
+            pick = pl.multiple_of((partners_ref[b, 1 + j] & (blocks - 1)) * size, size)
+            cat_ref[b, (2 + j) * size : (3 + j) * size, :] = far_ref[pl.ds(pick, size), :]
+
+
+def early_kernel(partners_ref, kv_ref, *refs):
+    fill(refs[-1], partners_ref, dict(zip(EARLY, refs[:-1], strict=True)), kv_ref)
+
+
+def main_kernel(far_count, q_heads, late, partners_ref, qd_ref, listed_ref, *refs):
+    far_refs, refs = refs[: len(late)], refs[len(late) :]
+    own_ref, probs_ref, dscores_ref, cat_ref = refs[:4]
+    part_refs = refs[4 : 4 + far_count]
+    (sums_ref,) = refs[4 + far_count :]
+    blocks = cat_ref.shape[0]
     slots = 2 + far_count
     size = BLOCK_TOKENS
     q_columns = q_heads * HEAD_SIZE
     pair = 2
-
-    for b in range(blocks):
-        rows = slice(b * size, (b + 1) * size)
-        near = kv_ref[(b - 1) * size : b * size, :] if b else far_refs[0][(blocks - 1) * size :, :]
-        cat_ref[b, :size, :] = kv_ref[rows, :]
-        cat_ref[b, size : 2 * size, :] = near
-        for j in range(far_count):
-            pick = pl.multiple_of((partners_ref[b, 1 + j] & (blocks - 1)) * size, size)
-            cat_ref[b, (2 + j) * size : (3 + j) * size, :] = far_refs[j][pl.ds(pick, size), :]
+    fill(cat_ref, partners_ref, dict(zip(late, far_refs, strict=True)))
 
     causal = lax.broadcasted_iota(jnp.int32, (size, size), 0) <= lax.broadcasted_iota(jnp.int32, (size, size), 1)
     causal = jnp.concatenate([causal] * pair, axis=1)
@@ -144,31 +172,44 @@
 
 def shards(query_projection, key_projection, value_projection, output_gradient, partners):
     heads = lax.axis_size("head")
-    kv = lax.all_to_all(pack(key_projection, value_projection, heads), "head", 0, 0, tiled=True)
-    qd = lax.all_to_all(pack(query_projection, output_gradient, heads), "head", 0, 0, tiled=True)
+    kv, qd = pack((key_projection, value_projection, query_projection, output_gradient), heads)
+    kv = lax.all_to_all(kv, "head", 0, 0, tiled=True)
+    qd = lax.all_to_all(qd, "head", 0, 0, tiled=True)
     kv = kv.reshape(-1, kv.shape[-1])
     qd = qd.reshape(-1, qd.shape[-1])
     tokens = kv.shape[0]
     blocks = tokens // BLOCK_TOKENS
     q_heads = qd.shape[1] // (2 * HEAD_SIZE)
     far_count = partners.shape[1] - 1
-    fars = [ring(kv, "seq", 2**j) for j in range(far_count)]
+    fars = {j: ring(kv, "seq", 2**j) for j in range(far_count) if j != 1}
+    fars[1] = ring(fars[0], "seq", 1)
+    late = (1, 4, 3)
     keys = (2 + far_count) * BLOCK_TOKENS
     big = (blocks, keys, q_heads * BLOCK_TOKENS)
+    cat_type = jax.ShapeDtypeStruct((blocks, keys, 2 * HEAD_SIZE), jnp.bfloat16)
+    listed = pl.pallas_call(
+        early_kernel,
+        out_shape=cat_type,
+        in_specs=[SMEM] + [VMEM] * (1 + len(EARLY)),
+        out_specs=VMEM,
+        cost_estimate=pl.CostEstimate(flops=10**10, transcendentals=0, bytes_accessed=0),
+        compiler_params=pltpu.CompilerParams(vmem_limit_bytes=8 << 20),
+    )(partners, kv, *[fars[j] for j in EARLY])
     own, probs, dscores, cat, *parts = pl.pallas_call(
-        functools.partial(main_kernel, far_count, q_heads),
+        functools.partial(main_kernel, far_count, q_heads, late),
         out_shape=[
             jax.ShapeDtypeStruct((tokens, 2 * HEAD_SIZE), jnp.float32),
             jax.ShapeDtypeStruct(big, jnp.bfloat16),
             jax.ShapeDtypeStruct(big, jnp.bfloat16),
-            jax.ShapeDtypeStruct((blocks, keys, 2 * HEAD_SIZE), jnp.bfloat16),
+            cat_type,
         ]
         + [jax.ShapeDtypeStruct((tokens, 2 * HEAD_SIZE), jnp.bfloat16)] * far_count,
-        in_specs=[SMEM] + [VMEM] * (2 + far_count),
+        in_specs=[SMEM] + [VMEM] * (2 + len(late)),
         out_specs=[VMEM] * (4 + far_count),
+        input_output_aliases={2: 3},
         scratch_shapes=[pltpu.VMEM((blocks, keys, 2 * HEAD_SIZE), jnp.float32)],
         compiler_params=pltpu.CompilerParams(vmem_limit_bytes=32 << 20),
-    )(partners, qd, kv, *fars)
+    )(partners, qd, listed, *[fars[j] for j in late])
     received = [ring(part, "seq", -(2**j)) for j, part in enumerate(parts)]
     attention, grad_query = pl.pallas_call(
         functools.partial(outputs_kernel, q_heads),

time: 67.1 us -> 59.4 us (0.89)
  waiting for transfers between devices: 22.8 us -> 10.7 us
  blocking collectives: 0 us -> 9.6 us
  local copies, waits for them, and re-layouts: 3.57 us -> 0.01 us
  starting transfers between devices: 31.2 us -> 27.9 us
  Pallas kernels: 8.43 us -> 9.64 us
    ppermute x10, waiting for transfers between devices: 20.8 us -> 10.7 us  [ring(): lax.ppermute(value, axis, [(s, (s + steps) % count) for s in range(count)])]
    all_to_all x0 -> x1, blocking collectives: none -> 9.6 us  [shards(): kv = lax.all_to_all(kv, 'head', 0, 0, tiled=True)]
    all_to_all x2 -> x1, starting transfers between devices: 9.78 us -> 4.86 us  [shards(): qd = lax.all_to_all(qd, 'head', 0, 0, tiled=True)]
    unnamed x10 -> x2, local copies, waits for them, and re-layouts: 3.57 us -> 0.01 us
    all_to_all x2 -> x1, waiting for transfers between devices: 1.94 us -> 0.01 us  [shards(): qd = lax.all_to_all(qd, 'head', 0, 0, tiled=True)]
    ppermute x10, starting transfers between devices: 21.5 us -> 23 us  [ring(): lax.ppermute(value, axis, [(s, (s + steps) % count) for s in range(count)])]
    pallas_call x3, Pallas kernels: 6.04 us -> 7.27 us  [the longest x1 4.42 us: shards(): pl.pallas_call(functools.partial(main_kernel, far_count, q_heads, late),...]
  transfers between devices with their start and end apart: 12 -> 11, of which waited for: 6 -> 4; matrix products, arithmetic and copies ran while one was open for 0% -> 0% of each run, Pallas kernels for 4% -> 4%
where the time goes in v2:
time: 59.4 us; the launch traced here: 58.5 us
  starting transfers between devices  27.9 us (47%)
  waiting for transfers between devices  10.7 us (18%)
  Pallas kernels  9.64 us (16%)
  blocking collectives  9.6 us (16%)
  between operations  0.68 us (1%)
    ppermute x10, starting transfers between devices, ring(): lax.ppermute(value, axis, [(s, (s + steps) % count) for s in range(count)])  23 us
    ppermute x10, waiting for transfers between devices, ring(): lax.ppermute(value, axis, [(s, (s + steps) % count) for s in range(count)])  10.7 us
    all_to_all x1, blocking collectives, shards(): kv = lax.all_to_all(kv, 'head', 0, 0, tiled=True)  9.6 us
    all_to_all x1, starting transfers between devices, shards(): qd = lax.all_to_all(qd, 'head', 0, 0, tiled=True)  4.86 us
    pallas_call x1, Pallas kernels, shards(): pl.pallas_call(functools.partial(main_kernel, far_count, q_heads, late),...  4.42 us
    pallas_call x1, Pallas kernels, pack(): pl.pallas_call(pack_kernel, out_shape=[packed(arrays[0]), packed(arrays[2...  2.27 us
    pallas_call x1, Pallas kernels, shards(): pl.pallas_call(functools.partial(outputs_kernel, q_heads), out_shape=[jax...  1.65 us
  transfers between devices with their start and end apart: 11, of which 4 were waited for; matrix products, arithmetic and copies ran while one was open for 0% of the time, Pallas kernels for 4%

profile of v2, /device:TPU:40, one launch (start us, length us, event | category | flops | bytes accessed | tf_op | source)
XLA Modules:
  0.0 58.5 jit_solution(12710216814221828038)
XLA Ops:
  0.6 0.0 copy-start
  0.6 2.3 %shard_map.84 = (bf16[8,32,256]{2,1,0:T(8,128)(2,1)}, bf16[8,32,1024]{2,1,0:T(8,128)(2,1)}) custom-call(bf16[32,1024]{1,0:T(8,128)(2,1)} %refs_0_.1, bf16[32,1024]{1,0:T(8,128)(2,1)} %refs_1_.1, bf16[32,4096]{1,0:T(8,128)(2,1)} %refs_2_.1, bf16[32,4096]{1,0:T(8,128)(2,1)} %refs_3_.1), custom_call_target="tpu_custom_call" | custom-call | tf_op jit(solution)/shard_map/pallas_call | solution.py:51
  2.9 9.6 %all_to_all.10 = bf16[8,32,256]{2,1,0:T(8,128)(2,1)S(1)} all-to-all(bf16[8,32,256]{2,1,0:T(8,128)(2,1)} %get-tuple-element.20), channel_id=1, replica_groups=mesh['seq'=32,'head'=8] {'head'}, dimensions={0} | all-to-all | bytes 262144 | tf_op jit(solution)/shard_map/all_to_all | solution.py:176
  12.5 1.9 %collective-permute-start.1 = (bf16[256,256]{1,0:T(8,128)(2,1)S(1)}, bf16[256,256]{1,0:T(8,128)(2,1)S(1)}, u32[]{:S(2)}, u32[]{:S(2)}) collective-permute-start(bf16[256,256]{1,0:T(8,128)(2,1)S(1)} %bitcast.3), channel_id=1, source_target_pairs={{0,8},{8,16},{16,24},{24,32},{32,40},{40,48},{48,56},{56,64},{64,7... | collective-permute-start | bytes 393224 | tf_op jit(solution)/shard_map/ppermute | solution.py:23
  14.4 5.4 %collective-permute-start = (bf16[256,256]{1,0:T(8,128)(2,1)S(1)}, bf16[256,256]{1,0:T(8,128)(2,1)S(1)}, u32[]{:S(2)}, u32[]{:S(2)}) collective-permute-start(bf16[256,256]{1,0:T(8,128)(2,1)S(1)} %bitcast.4), channel_id=1, source_target_pairs={{0,32},{8,40},{16,48},{24,56},{32,64},{40,72},{48,80},{56,88},{64,... | collective-permute-start | bytes 393224 | tf_op jit(solution)/shard_map/ppermute | solution.py:23
  19.8 4.9 %all-to-all-start = ((bf16[8,32,1024]{2,1,0:T(8,128)(2,1)}), bf16[8,32,1024]{2,1,0:T(8,128)(2,1)S(1)}, u32[]{:S(2)}, u32[]{:S(2)}) async-start(bf16[8,32,1024]{2,1,0:T(8,128)(2,1)} %get-tuple-element.19), calls=%async_computation | async-start | bytes 1048576 | tf_op jit(solution)/shard_map/all_to_all | solution.py:177
  24.7 1.5 %collective-permute-start.4 = (bf16[256,256]{1,0:T(8,128)(2,1)S(1)}, bf16[256,256]{1,0:T(8,128)(2,1)S(1)}, u32[]{:S(2)}, u32[]{:S(2)}) collective-permute-start(bf16[256,256]{1,0:T(8,128)(2,1)S(1)} %bitcast.5), channel_id=1, source_target_pairs={{0,64},{8,72},{16,80},{24,88},{32,96},{40,104},{48,112},{56,120},{... | collective-permute-start | bytes 393224 | tf_op jit(solution)/shard_map/ppermute | solution.py:23
  26.2 2.7 %collective-permute-start.3 = (bf16[256,256]{1,0:T(8,128)(2,1)S(1)}, bf16[256,256]{1,0:T(8,128)(2,1)S(1)}, u32[]{:S(2)}, u32[]{:S(2)}) collective-permute-start(bf16[256,256]{1,0:T(8,128)(2,1)S(1)} %bitcast.6), channel_id=1, source_target_pairs={{0,128},{8,136},{16,144},{24,152},{32,160},{40,168},{48,176},{56,1... | collective-permute-start | bytes 393224 | tf_op jit(solution)/shard_map/ppermute | solution.py:23
  28.9 0.0 collective-permute-done.1.refs_1_
  28.9 1.0 %collective-permute-start.2 = (bf16[256,256]{1,0:T(8,128)(2,1)S(1)}, bf16[256,256]{1,0:T(8,128)(2,1)S(1)}, u32[]{:S(2)}, u32[]{:S(2)}) collective-permute-start(bf16[256,256]{1,0:T(8,128)(2,1)S(1)} %collective-permute-done.1.refs_1_), channel_id=1, source_target_pairs={{0,8},{8,16},{16,24},{24,32},{32,40},{40,48},{48,56},{56,64},{64,7... | collective-permute-start | bytes 393224 | tf_op jit(solution)/shard_map/ppermute | solution.py:23
  29.9 0.0 collective-permute-done.refs_0_
  29.9 0.0 copy-done
  29.9 0.6 shard_map.85.listed_ref
  30.5 0.9 %collective-permute-done.4.refs_2_ = bf16[256,256]{1,0:T(8,128)(2,1)S(1)} collective-permute-done((bf16[256,256]{1,0:T(8,128)(2,1)S(1)}, bf16[256,256]{1,0:T(8,128)(2,1)S(1)}, u32[]{:S(2)}, u32[]{:S(2)}) %collective-permute-start.4) | collective-permute-done | bytes 131104 | tf_op jit(solution)/shard_map/ppermute | solution.py:23
  31.5 3.8 %collective-permute-done.3.refs_1_ = bf16[256,256]{1,0:T(8,128)(2,1)S(1)} collective-permute-done((bf16[256,256]{1,0:T(8,128)(2,1)S(1)}, bf16[256,256]{1,0:T(8,128)(2,1)S(1)}, u32[]{:S(2)}, u32[]{:S(2)}) %collective-permute-start.3) | collective-permute-done | bytes 131104 | tf_op jit(solution)/shard_map/ppermute | solution.py:23
  35.2 0.0 collective-permute-done.2.refs_0_
  35.2 0.0 all-to-all-done
  35.3 4.4 %shard_map.86 = (f32[256,256]{1,0:T(8,128)S(1)}, bf16[2,896,512]{2,1,0:T(8,128)(2,1)S(1)}, bf16[2,896,512]{2,1,0:T(8,128)(2,1)S(1)}, bf16[2,896,256]{2,1,0:T(8,1...) custom-call(s32[2,6]{1,0:T(2,128)S(1)} %copy-done, ...), custom_call_target="tpu_custom_call", output_to_operand_aliasing={{3}: (2, {})} | custom-call | tf_op jit(solution)/shard_map/pallas_call | solution.py:198
  39.7 4.1 %collective-permute-start.5 = (bf16[256,256]{1,0:T(8,128)(2,1)S(1)}, bf16[256,256]{1,0:T(8,128)(2,1)S(1)}, u32[]{:S(2)}, u32[]{:S(2)}) collective-permute-start(bf16[256,256]{1,0:T(8,128)(2,1)S(1)} %get-tuple-element.27), channel_id=1, source_target_pairs={{0,248},{8,0},{16,8},{24,16},{32,24},{40,32},{48,40},{56,48},{64,5... | collective-permute-start | bytes 393224 | tf_op jit(solution)/shard_map/ppermute | solution.py:23
  43.8 0.0 collective-permute-start.6
  43.8 2.5 %collective-permute-start.7 = (bf16[256,256]{1,0:T(8,128)(2,1)S(1)}, bf16[256,256]{1,0:T(8,128)(2,1)S(1)}, u32[]{:S(2)}, u32[]{:S(2)}) collective-permute-start(bf16[256,256]{1,0:T(8,128)(2,1)S(1)} %get-tuple-element.29), channel_id=1, source_target_pairs={{0,224},{8,232},{16,240},{24,248},{32,0},{40,8},{48,16},{56,24},{6... | collective-permute-start | bytes 393224 | tf_op jit(solution)/shard_map/ppermute | solution.py:23
  46.4 1.1 %collective-permute-start.8 = (bf16[256,256]{1,0:T(8,128)(2,1)S(1)}, bf16[256,256]{1,0:T(8,128)(2,1)S(1)}, u32[]{:S(2)}, u32[]{:S(2)}) collective-permute-start(bf16[256,256]{1,0:T(8,128)(2,1)S(1)} %get-tuple-element.30), channel_id=1, source_target_pairs={{0,192},{8,200},{16,208},{24,216},{32,224},{40,232},{48,240},{56,2... | collective-permute-start | bytes 393224 | tf_op jit(solution)/shard_map/ppermute | solution.py:23
  47.5 2.7 %collective-permute-start.9 = (bf16[256,256]{1,0:T(8,128)(2,1)S(1)}, bf16[256,256]{1,0:T(8,128)(2,1)S(1)}, u32[]{:S(2)}, u32[]{:S(2)}) collective-permute-start(bf16[256,256]{1,0:T(8,128)(2,1)S(1)} %get-tuple-element.31), channel_id=1, source_target_pairs={{0,128},{8,136},{16,144},{24,152},{32,160},{40,168},{48,176},{56,1... | collective-permute-start | bytes 393224 | tf_op jit(solution)/shard_map/ppermute | solution.py:23
  50.2 1.6 %shard_map.87 = (bf16[256,512]{1,0:T(8,128)(2,1)}, bf16[256,512]{1,0:T(8,128)(2,1)}) custom-call(bf16[2,896,512]{2,1,0:T(8,128)(2,1)S(1)} %get-tuple-element.21.probs_ref, bf16[2,896,512]{2,1,0:T(8,128)(2,1)S(1)} %get-tuple-element.22.dscores_ref, bf16[2,896,256]{2,1,0:T(8,128)(2,1)S(1)} %get-tuple-element.23.cat_ref), custom_call_target="tpu_custom_call" | custom-call | tf_op jit(solution)/shard_map/pallas_call | solution.py:214
  51.8 0.0 collective-permute-done.5.refs_0_
  51.8 3.6 %collective-permute-done.6.refs_1_ = bf16[256,256]{1,0:T(8,128)(2,1)S(1)} collective-permute-done((bf16[256,256]{1,0:T(8,128)(2,1)S(1)}, bf16[256,256]{1,0:T(8,128)(2,1)S(1)}, u32[]{:S(2)}, u32[]{:S(2)}) %collective-permute-start.6) | collective-permute-done | bytes 131104 | tf_op jit(solution)/shard_map/ppermute | solution.py:23
  55.4 2.4 %collective-permute-done.7.refs_2_ = bf16[256,256]{1,0:T(8,128)(2,1)S(1)} collective-permute-done((bf16[256,256]{1,0:T(8,128)(2,1)S(1)}, bf16[256,256]{1,0:T(8,128)(2,1)S(1)}, u32[]{:S(2)}, u32[]{:S(2)}) %collective-permute-start.7) | collective-permute-done | bytes 131104 | tf_op jit(solution)/shard_map/ppermute | solution.py:23
  57.8 0.0 collective-permute-done.8.refs_3_
  57.8 0.0 collective-permute-done.9.refs_4_
  57.8 0.7 %shard_map.88 = (bf16[256,128]{1,0:T(8,128)(2,1)}, bf16[256,128]{1,0:T(8,128)(2,1)}) custom-call(f32[256,256]{1,0:T(8,128)S(1)} %get-tuple-element.26.own_ref, bf16[256,256]{1,0:T(8,128)(2,1)S(1)} %collective-permute-done.5.refs_0_, bf16[256,256]{1,0:T(8,128)(2,1)S(1)} %collective-permute-done.6.refs_1_, ...), custom_call_target="tpu_custom_call" | custom-call | tf_op jit(solution)/shard_map/pallas_call | solution.py:221
Async XLA Ops:
  0.6 29.3 %copy-start = (s32[2,6]{1,0:T(2,128)S(1)}, s32[2,6]{1,0:T(2,128)}, u32[]{:S(2)}) copy-start(s32[2,6]{1,0:T(2,128)} %partners_ref.3) | copy-start | bytes 148
  12.5 16.4 %collective-permute-start.1 = (bf16[256,256]{1,0:T(8,128)(2,1)S(1)}, bf16[256,256]{1,0:T(8,128)(2,1)S(1)}, u32[]{:S(2)}, u32[]{:S(2)}) collective-permute-start(bf16[256,256]{1,0:T(8,128)(2,1)S(1)} %bitcast.3), channel_id=1, source_target_pairs={{0,8},{8,16},{16,24},{24,32},{32,40},{40,48},{48,56},{56,64},{64,7... | collective-permute-start | bytes 393224 | tf_op jit(solution)/shard_map/ppermute | solution.py:23
  14.4 15.5 %collective-permute-start = (bf16[256,256]{1,0:T(8,128)(2,1)S(1)}, bf16[256,256]{1,0:T(8,128)(2,1)S(1)}, u32[]{:S(2)}, u32[]{:S(2)}) collective-permute-start(bf16[256,256]{1,0:T(8,128)(2,1)S(1)} %bitcast.4), channel_id=1, source_target_pairs={{0,32},{8,40},{16,48},{24,56},{32,64},{40,72},{48,80},{56,88},{64,... | collective-permute-start | bytes 393224 | tf_op jit(solution)/shard_map/ppermute | solution.py:23
  19.8 15.4 %all-to-all-start = ((bf16[8,32,1024]{2,1,0:T(8,128)(2,1)}), bf16[8,32,1024]{2,1,0:T(8,128)(2,1)S(1)}, u32[]{:S(2)}, u32[]{:S(2)}) async-start(bf16[8,32,1024]{2,1,0:T(8,128)(2,1)} %get-tuple-element.19), calls=%async_computation | async-start | bytes 1048576 | tf_op jit(solution)/shard_map/all_to_all | solution.py:177
  24.7 6.8 %collective-permute-start.4 = (bf16[256,256]{1,0:T(8,128)(2,1)S(1)}, bf16[256,256]{1,0:T(8,128)(2,1)S(1)}, u32[]{:S(2)}, u32[]{:S(2)}) collective-permute-start(bf16[256,256]{1,0:T(8,128)(2,1)S(1)} %bitcast.5), channel_id=1, source_target_pairs={{0,64},{8,72},{16,80},{24,88},{32,96},{40,104},{48,112},{56,120},{... | collective-permute-start | bytes 393224 | tf_op jit(solution)/shard_map/ppermute | solution.py:23
  26.2 9.1 %collective-permute-start.3 = (bf16[256,256]{1,0:T(8,128)(2,1)S(1)}, bf16[256,256]{1,0:T(8,128)(2,1)S(1)}, u32[]{:S(2)}, u32[]{:S(2)}) collective-permute-start(bf16[256,256]{1,0:T(8,128)(2,1)S(1)} %bitcast.6), channel_id=1, source_target_pairs={{0,128},{8,136},{16,144},{24,152},{32,160},{40,168},{48,176},{56,1... | collective-permute-start | bytes 393224 | tf_op jit(solution)/shard_map/ppermute | solution.py:23
  28.9 6.3 %collective-permute-start.2 = (bf16[256,256]{1,0:T(8,128)(2,1)S(1)}, bf16[256,256]{1,0:T(8,128)(2,1)S(1)}, u32[]{:S(2)}, u32[]{:S(2)}) collective-permute-start(bf16[256,256]{1,0:T(8,128)(2,1)S(1)} %collective-permute-done.1.refs_1_), channel_id=1, source_target_pairs={{0,8},{8,16},{16,24},{24,32},{32,40},{40,48},{48,56},{56,64},{64,7... | collective-permute-start | bytes 393224 | tf_op jit(solution)/shard_map/ppermute | solution.py:23
  39.7 12.1 %collective-permute-start.5 = (bf16[256,256]{1,0:T(8,128)(2,1)S(1)}, bf16[256,256]{1,0:T(8,128)(2,1)S(1)}, u32[]{:S(2)}, u32[]{:S(2)}) collective-permute-start(bf16[256,256]{1,0:T(8,128)(2,1)S(1)} %get-tuple-element.27), channel_id=1, source_target_pairs={{0,248},{8,0},{16,8},{24,16},{32,24},{40,32},{48,40},{56,48},{64,5... | collective-permute-start | bytes 393224 | tf_op jit(solution)/shard_map/ppermute | solution.py:23
  43.8 11.6 %collective-permute-start.6 = (bf16[256,256]{1,0:T(8,128)(2,1)S(1)}, bf16[256,256]{1,0:T(8,128)(2,1)S(1)}, u32[]{:S(2)}, u32[]{:S(2)}) collective-permute-start(bf16[256,256]{1,0:T(8,128)(2,1)S(1)} %get-tuple-element.28), channel_id=1, source_target_pairs={{0,240},{8,248},{16,0},{24,8},{32,16},{40,24},{48,32},{56,40},{64,... | collective-permute-start | bytes 393224 | tf_op jit(solution)/shard_map/ppermute | solution.py:23
  43.8 14.0 %collective-permute-start.7 = (bf16[256,256]{1,0:T(8,128)(2,1)S(1)}, bf16[256,256]{1,0:T(8,128)(2,1)S(1)}, u32[]{:S(2)}, u32[]{:S(2)}) collective-permute-start(bf16[256,256]{1,0:T(8,128)(2,1)S(1)} %get-tuple-element.29), channel_id=1, source_target_pairs={{0,224},{8,232},{16,240},{24,248},{32,0},{40,8},{48,16},{56,24},{6... | collective-permute-start | bytes 393224 | tf_op jit(solution)/shard_map/ppermute | solution.py:23
  46.4 11.4 %collective-permute-start.8 = (bf16[256,256]{1,0:T(8,128)(2,1)S(1)}, bf16[256,256]{1,0:T(8,128)(2,1)S(1)}, u32[]{:S(2)}, u32[]{:S(2)}) collective-permute-start(bf16[256,256]{1,0:T(8,128)(2,1)S(1)} %get-tuple-element.30), channel_id=1, source_target_pairs={{0,192},{8,200},{16,208},{24,216},{32,224},{40,232},{48,240},{56,2... | collective-permute-start | bytes 393224 | tf_op jit(solution)/shard_map/ppermute | solution.py:23
  47.5 10.3 %collective-permute-start.9 = (bf16[256,256]{1,0:T(8,128)(2,1)S(1)}, bf16[256,256]{1,0:T(8,128)(2,1)S(1)}, u32[]{:S(2)}, u32[]{:S(2)}) collective-permute-start(bf16[256,256]{1,0:T(8,128)(2,1)S(1)} %get-tuple-element.31), channel_id=1, source_target_pairs={{0,128},{8,136},{16,144},{24,152},{32,160},{40,168},{48,176},{56,1... | collective-permute-start | bytes 393224 | tf_op jit(solution)/shard_map/ppermute | solution.py:23

commit v3 on v2

--- a/solution.py
+++ b/solution.py
@@ -23,37 +23,55 @@
     return lax.ppermute(value, axis, [(s, (s + steps) % count) for s in range(count)])
 
 
+def line(value, axis, steps):
+    count = lax.axis_size(axis)
+    pairs = [(s, s + steps) for s in range(count) if 0 <= s + steps < count]
+    return lax.ppermute(value, axis, pairs)
+
+
 def pack_kernel(*refs):
-    sources, packed, sems = refs[:4], refs[4:6], refs[6]
+    sources, packed, held = refs[:4], refs[4:6], refs[6:8]
+    in_sems, out_sems = refs[8:]
     heads = packed[0].shape[0]
-    copies = []
-    for i, source in enumerate(sources):
-        target = packed[i // 2]
-        width = source.shape[1] // heads
+
+    def arrival(i, head):
+        width = sources[i].shape[1] // heads
+        return pltpu.make_async_copy(
+            sources[i].at[:, pl.ds(head * width, width)],
+            held[i // 2].at[head, :, pl.ds((i % 2) * width, width)],
+            in_sems.at[i, head],
+        )
+
+    def departure(k, head):
+        return pltpu.make_async_copy(held[k].at[head], packed[k].at[head], out_sems.at[k, head])
+
+    for k in range(2):
         for head in range(heads):
-            copies.append(
-                pltpu.make_async_copy(
-                    source.at[:, pl.ds(head * width, width)],
-                    target.at[head, :, pl.ds((i % 2) * width, width)],
-                    sems.at[i, head],
-                )
-            )
-    for copy in copies:
-        copy.start()
-    for copy in copies:
-        copy.wait()
+            arrival(2 * k, head).start()
+            arrival(2 * k + 1, head).start()
+    for k in range(2):
+        for head in range(heads):
+            arrival(2 * k, head).wait()
+            arrival(2 * k + 1, head).wait()
+            departure(k, head).start()
+    for k in range(2):
+        for head in range(heads):
+            departure(k, head).wait()
 
 
 def pack(arrays, heads):
-    def packed(array):
-        return jax.ShapeDtypeStruct((heads, array.shape[0], 2 * array.shape[1] // heads), array.dtype)
-
+    shapes = [(heads, a.shape[0], 2 * a.shape[1] // heads) for a in (arrays[0], arrays[2])]
+    dtype = arrays[0].dtype
     return pl.pallas_call(
         pack_kernel,
-        out_shape=[packed(arrays[0]), packed(arrays[2])],
+        out_shape=[jax.ShapeDtypeStruct(shape, dtype) for shape in shapes],
         in_specs=[HBM] * 4,
-        out_specs=[VMEM] * 2,
-        scratch_shapes=[pltpu.SemaphoreType.DMA((4, heads))],
+        out_specs=[HBM] * 2,
+        scratch_shapes=[
+            *[pltpu.VMEM(shape, dtype) for shape in shapes],
+            pltpu.SemaphoreType.DMA((4, heads)),
+            pltpu.SemaphoreType.DMA((2, heads)),
+        ],
         compiler_params=pltpu.CompilerParams(vmem_limit_bytes=60 << 20),
     )(*arrays)
 
@@ -81,11 +99,25 @@
     fill(refs[-1], partners_ref, dict(zip(EARLY, refs[:-1], strict=True)), kv_ref)
 
 
+def stack(qd_ref, b, first, heads):
+    rows = slice(b * BLOCK_TOKENS, (b + 1) * BLOCK_TOKENS)
+    columns = [slice((first + h) * HEAD_SIZE, (first + h + 1) * HEAD_SIZE) for h in range(heads)]
+    return jnp.concatenate([qd_ref[rows, c] for c in columns], axis=0)
+
+
+def gradients(probs_ref, dscores_ref, qd_ref, sums_ref, q_heads, b, low, high):
+    rows = slice(low * BLOCK_TOKENS, high * BLOCK_TOKENS)
+    query = stack(qd_ref, b, 0, q_heads)
+    cotangent = stack(qd_ref, b, q_heads, q_heads)
+    sums_ref[b, rows, :HEAD_SIZE] = SCALING * dot(dscores_ref[b, rows, :], query, (1, 0))
+    sums_ref[b, rows, HEAD_SIZE:] = dot(probs_ref[b, rows, :], cotangent, (1, 0))
+
+
 def main_kernel(far_count, q_heads, late, partners_ref, qd_ref, listed_ref, *refs):
     far_refs, refs = refs[: len(late)], refs[len(late) :]
-    own_ref, probs_ref, dscores_ref, cat_ref = refs[:4]
-    part_refs = refs[4 : 4 + far_count]
-    (sums_ref,) = refs[4 + far_count :]
+    probs_ref, dscores_ref, cat_ref = refs[:3]
+    part_refs = refs[3 : 3 + far_count]
+    (sums_ref,) = refs[3 + far_count :]
     blocks = cat_ref.shape[0]
     slots = 2 + far_count
     size = BLOCK_TOKENS
@@ -113,7 +145,7 @@
             scores += [raw[(1 + l) * size : (2 + l) * size] + bias[l] for l in range(1 + far_count)]
             top = functools.reduce(jnp.maximum, scores)
             top = jnp.max(top, axis=0, keepdims=True)
-            weights = [jnp.exp((s - top) * SCALING) for s in scores]
+            weights = [jnp.exp2((s - top) * (SCALING * math.log2(math.e))) for s in scores]
             total = jnp.sum(functools.reduce(jnp.add, weights), axis=0, keepdims=True)
             inverse = 1.0 / total
             dprobs = dot(values, cotangent, (1, 1))
@@ -127,14 +159,7 @@
             for i in range(slots):
                 change = weights[i] * (dprobs[i * size : (i + 1) * size] - row_dot)
                 dscores_ref[b, i * size : (i + 1) * size, columns] = change.astype(jnp.bfloat16)
-        sums_ref[b, :, :HEAD_SIZE] = SCALING * dot(dscores_ref[b], jnp.concatenate(queries, axis=0), (1, 0))
-        sums_ref[b, :, HEAD_SIZE:] = dot(probs_ref[b], jnp.concatenate(cotangents, axis=0), (1, 0))
-
-    for b in range(blocks):
-        total = sums_ref[b, :size, :]
-        if b + 1 < blocks:
-            total = total + sums_ref[b + 1, size : 2 * size, :]
-        own_ref[b * size : (b + 1) * size, :] = total
+        gradients(probs_ref, dscores_ref, qd_ref, sums_ref, q_heads, b, 2 if b else 1, slots)
     for j in range(far_count):
         at = slice((2 + j) * size, (3 + j) * size)
         for target in range(blocks):
@@ -148,9 +173,10 @@
             part_refs[j][target * size : (target + 1) * size, :] = total.astype(jnp.bfloat16)
 
 
-def outputs_kernel(q_heads, probs_ref, dscores_ref, cat_ref, attention_ref, grad_query_ref):
+def outputs_kernel(q_heads, qd_ref, probs_ref, dscores_ref, cat_ref, attention_ref, grad_query_ref, own_ref, sums_ref):
     size = BLOCK_TOKENS
-    for b in range(probs_ref.shape[0]):
+    blocks = probs_ref.shape[0]
+    for b in range(blocks):
         rows = slice(b * size, (b + 1) * size)
         attention = dot(cat_ref[b, :, HEAD_SIZE:], probs_ref[b], (0, 0))
         grad_query = SCALING * dot(cat_ref[b, :, :HEAD_SIZE], dscores_ref[b], (0, 0))
@@ -159,6 +185,12 @@
             at = slice(h * size, (h + 1) * size)
             attention_ref[rows, columns] = attention[:, at].T.astype(jnp.bfloat16)
             grad_query_ref[rows, columns] = grad_query[:, at].T.astype(jnp.bfloat16)
+        gradients(probs_ref, dscores_ref, qd_ref, sums_ref, q_heads, b, 0, 2 if b else 1)
+    for b in range(blocks):
+        total = sums_ref[b, :size, :]
+        if b + 1 < blocks:
+            total = total + sums_ref[b + 1, size : 2 * size, :]
+        own_ref[b * size : (b + 1) * size, :] = total
 
 
 def sum_kernel(own_ref, *refs):
@@ -181,7 +213,7 @@
     blocks = tokens // BLOCK_TOKENS
     q_heads = qd.shape[1] // (2 * HEAD_SIZE)
     far_count = partners.shape[1] - 1
-    fars = {j: ring(kv, "seq", 2**j) for j in range(far_count) if j != 1}
+    fars = {j: (line if j in (4,) else ring)(kv, "seq", 2**j) for j in range(far_count) if j != 1}
     fars[1] = ring(fars[0], "seq", 1)
     late = (1, 4, 3)
     keys = (2 + far_count) * BLOCK_TOKENS
@@ -195,29 +227,30 @@
         cost_estimate=pl.CostEstimate(flops=10**10, transcendentals=0, bytes_accessed=0),
         compiler_params=pltpu.CompilerParams(vmem_limit_bytes=8 << 20),
     )(partners, kv, *[fars[j] for j in EARLY])
-    own, probs, dscores, cat, *parts = pl.pallas_call(
+    probs, dscores, cat, *parts = pl.pallas_call(
         functools.partial(main_kernel, far_count, q_heads, late),
         out_shape=[
-            jax.ShapeDtypeStruct((tokens, 2 * HEAD_SIZE), jnp.float32),
             jax.ShapeDtypeStruct(big, jnp.bfloat16),
             jax.ShapeDtypeStruct(big, jnp.bfloat16),
             cat_type,
         ]
         + [jax.ShapeDtypeStruct((tokens, 2 * HEAD_SIZE), jnp.bfloat16)] * far_count,
         in_specs=[SMEM] + [VMEM] * (2 + len(late)),
-        out_specs=[VMEM] * (4 + far_count),
-        input_output_aliases={2: 3},
+        out_specs=[VMEM] * (3 + far_count),
+        input_output_aliases={2: 2},
         scratch_shapes=[pltpu.VMEM((blocks, keys, 2 * HEAD_SIZE), jnp.float32)],
         compiler_params=pltpu.CompilerParams(vmem_limit_bytes=32 << 20),
     )(partners, qd, listed, *[fars[j] for j in late])
-    received = [ring(part, "seq", -(2**j)) for j, part in enumerate(parts)]
-    attention, grad_query = pl.pallas_call(
+    received = [(line if j in (4,) else ring)(part, "seq", -(2**j)) for j, part in enumerate(parts)]
+    attention, grad_query, own = pl.pallas_call(
         functools.partial(outputs_kernel, q_heads),
-        out_shape=[jax.ShapeDtypeStruct((tokens, q_heads * HEAD_SIZE), jnp.bfloat16)] * 2,
-        in_specs=[VMEM] * 3,
-        out_specs=[VMEM] * 2,
+        out_shape=[jax.ShapeDtypeStruct((tokens, q_heads * HEAD_SIZE), jnp.bfloat16)] * 2
+        + [jax.ShapeDtypeStruct((tokens, 2 * HEAD_SIZE), jnp.float32)],
+        in_specs=[VMEM] * 4,
+        out_specs=[VMEM] * 3,
+        scratch_shapes=[pltpu.VMEM((blocks, 2 * BLOCK_TOKENS, 2 * HEAD_SIZE), jnp.float32)],
         compiler_params=pltpu.CompilerParams(vmem_limit_bytes=32 << 20),
-    )(probs, dscores, cat)
+    )(qd, probs, dscores, cat)
     key_gradient, value_gradient = pl.pallas_call(
         sum_kernel,
         out_shape=[jax.ShapeDtypeStruct((tokens, HEAD_SIZE), jnp.bfloat16)] * 2,

time: 59.4 us -> 58.5 us (0.985)
  waiting for transfers between devices: 10.7 us -> 9.67 us
  starting transfers between devices: 27.9 us -> 28.5 us
    ppermute x0 -> x2, starting transfers between devices: none -> 5.91 us  [line(): return lax.ppermute(value, axis, pairs)]
    ppermute x10 -> x8, starting transfers between devices: 23 us -> 17.7 us  [ring(): lax.ppermute(value, axis, [(s, (s + steps) % count) for s in range(count)])]
    ppermute x10 -> x8, waiting for transfers between devices: 10.7 us -> 8.62 us  [ring(): lax.ppermute(value, axis, [(s, (s + steps) % count) for s in range(count)])]
    ppermute x0 -> x2, waiting for transfers between devices: none -> 1.05 us  [line(): return lax.ppermute(value, axis, pairs)]
  transfers between devices with their start and end apart: 11 -> 11, of which waited for: 4 -> 5; matrix products, arithmetic and copies ran while one was open for 0% -> 0% of each run, Pallas kernels for 4% -> 4%
where the time goes in v3:
time: 58.5 us; the launch traced here: 57.9 us
  starting transfers between devices  28.5 us (49%)
  waiting for transfers between devices  9.67 us (17%)
  blocking collectives  9.6 us (16%)
  Pallas kernels  9.44 us (16%)
  between operations  0.71 us (1%)
    ppermute x8, starting transfers between devices, ring(): lax.ppermute(value, axis, [(s, (s + steps) % count) for s in range(count)])  17.7 us
    all_to_all x1, blocking collectives, shards(): kv = lax.all_to_all(kv, 'head', 0, 0, tiled=True)  9.6 us
    ppermute x8, waiting for transfers between devices, ring(): lax.ppermute(value, axis, [(s, (s + steps) % count) for s in range(count)])  8.62 us
    ppermute x2, starting transfers between devices, line(): return lax.ppermute(value, axis, pairs)  5.91 us
    all_to_all x1, starting transfers between devices, shards(): qd = lax.all_to_all(qd, 'head', 0, 0, tiled=True)  4.86 us
    pallas_call x1, Pallas kernels, shards(): pl.pallas_call(functools.partial(main_kernel, far_count, q_heads, late),...  4.21 us
    pallas_call x1, Pallas kernels, pack(): pl.pallas_call(pack_kernel, out_shape=[jax.ShapeDtypeStruct(shape, dtype)...  2.2 us
    pallas_call x1, Pallas kernels, shards(): pl.pallas_call(functools.partial(outputs_kernel, q_heads), out_shape=[jax...  1.72 us
  transfers between devices with their start and end apart: 11, of which 5 were waited for; matrix products, arithmetic and copies ran while one was open for 0% of the time, Pallas kernels for 4%

profile of v3, /device:TPU:40, one launch (start us, length us, event | category | flops | bytes accessed | tf_op | source)
XLA Modules:
  0.0 57.9 jit_solution(11188160643260905017)
XLA Ops:
  0.6 0.0 copy-start
  0.6 2.2 %shard_map.84 = (bf16[8,32,256]{2,1,0:T(8,128)(2,1)}, bf16[8,32,1024]{2,1,0:T(8,128)(2,1)}) custom-call(bf16[32,1024]{1,0:T(8,128)(2,1)} %refs_0_.1, bf16[32,1024]{1,0:T(8,128)(2,1)} %refs_1_.1, bf16[32,4096]{1,0:T(8,128)(2,1)} %refs_2_.1, bf16[32,4096]{1,0:T(8,128)(2,1)} %refs_3_.1), custom_call_target="tpu_custom_call" | custom-call | tf_op jit(solution)/shard_map/pallas_call | solution.py:65
  2.8 9.6 %all_to_all.10 = bf16[8,32,256]{2,1,0:T(8,128)(2,1)S(1)} all-to-all(bf16[8,32,256]{2,1,0:T(8,128)(2,1)} %get-tuple-element.20), channel_id=1, replica_groups=mesh['seq'=32,'head'=8] {'head'}, dimensions={0} | all-to-all | bytes 262144 | tf_op jit(solution)/shard_map/all_to_all | solution.py:208
  12.4 1.9 %collective-permute-start.1 = (bf16[256,256]{1,0:T(8,128)(2,1)S(1)}, bf16[256,256]{1,0:T(8,128)(2,1)S(1)}, u32[]{:S(2)}, u32[]{:S(2)}) collective-permute-start(bf16[256,256]{1,0:T(8,128)(2,1)S(1)} %bitcast.4), channel_id=1, source_target_pairs={{0,8},{8,16},{16,24},{24,32},{32,40},{40,48},{48,56},{56,64},{64,7... | collective-permute-start | bytes 393224 | tf_op jit(solution)/shard_map/ppermute | solution.py:23
  14.4 5.4 %collective-permute-start = (bf16[256,256]{1,0:T(8,128)(2,1)S(1)}, bf16[256,256]{1,0:T(8,128)(2,1)S(1)}, u32[]{:S(2)}, u32[]{:S(2)}) collective-permute-start(bf16[256,256]{1,0:T(8,128)(2,1)S(1)} %bitcast.5), channel_id=1, source_target_pairs={{0,32},{8,40},{16,48},{24,56},{32,64},{40,72},{48,80},{56,88},{64,... | collective-permute-start | bytes 393224 | tf_op jit(solution)/shard_map/ppermute | solution.py:23
  19.8 4.9 %all-to-all-start = ((bf16[8,32,1024]{2,1,0:T(8,128)(2,1)}), bf16[8,32,1024]{2,1,0:T(8,128)(2,1)S(1)}, u32[]{:S(2)}, u32[]{:S(2)}) async-start(bf16[8,32,1024]{2,1,0:T(8,128)(2,1)} %get-tuple-element.19), calls=%async_computation | async-start | bytes 1048576 | tf_op jit(solution)/shard_map/all_to_all | solution.py:209
  24.6 1.5 %collective-permute-start.4 = (bf16[256,256]{1,0:T(8,128)(2,1)S(1)}, bf16[256,256]{1,0:T(8,128)(2,1)S(1)}, u32[]{:S(2)}, u32[]{:S(2)}) collective-permute-start(bf16[256,256]{1,0:T(8,128)(2,1)S(1)} %bitcast.6), channel_id=1, source_target_pairs={{0,64},{8,72},{16,80},{24,88},{32,96},{40,104},{48,112},{56,120},{... | collective-permute-start | bytes 393224 | tf_op jit(solution)/shard_map/ppermute | solution.py:23
  26.1 4.6 %collective-permute-start.3 = (bf16[256,256]{1,0:T(8,128)(2,1)S(1)}, bf16[256,256]{1,0:T(8,128)(2,1)S(1)}, u32[]{:S(2)}, u32[]{:S(2)}) collective-permute-start(bf16[256,256]{1,0:T(8,128)(2,1)S(1)} %bitcast.7), channel_id=1, source_target_pairs={{0,128},{8,136},{16,144},{24,152},{32,160},{40,168},{48,176},{56,1... | collective-permute-start | bytes 393224 | tf_op jit(solution)/shard_map/ppermute | solution.py:29
  30.7 0.0 collective-permute-done.1.refs_1_
  30.8 1.1 %collective-permute-start.2 = (bf16[256,256]{1,0:T(8,128)(2,1)S(1)}, bf16[256,256]{1,0:T(8,128)(2,1)S(1)}, u32[]{:S(2)}, u32[]{:S(2)}) collective-permute-start(bf16[256,256]{1,0:T(8,128)(2,1)S(1)} %collective-permute-done.1.refs_1_), channel_id=1, source_target_pairs={{0,8},{8,16},{16,24},{24,32},{32,40},{40,48},{48,56},{56,64},{64,7... | collective-permute-start | bytes 393224 | tf_op jit(solution)/shard_map/ppermute | solution.py:23
  31.9 0.0 collective-permute-done.refs_0_
  31.9 0.0 copy-done
  31.9 0.6 %shard_map.85.listed_ref = bf16[2,896,256]{2,1,0:T(8,128)(2,1)S(1)} custom-call(s32[2,6]{1,0:T(2,128)S(1)} %copy-done, bf16[256,256]{1,0:T(8,128)(2,1)S(1)} %bitcast.8, bf16[256,256]{1,0:T(8,128)(2,1)S(1)} %collective-permute-done.refs_0_, bf16[256,256]{1,0:T(8,128)(2,1)S(1)} %collective-permute-done.1.refs_1_), custom_call_target="tpu_custom_call" | custom-call | flops 10000000000 | tf_op jit(solution)/shard_map/pallas_call | solution.py:222
  32.5 0.0 collective-permute-done.4.refs_2_
  32.5 1.0 %collective-permute-done.3.refs_1_ = bf16[256,256]{1,0:T(8,128)(2,1)S(1)} collective-permute-done((bf16[256,256]{1,0:T(8,128)(2,1)S(1)}, bf16[256,256]{1,0:T(8,128)(2,1)S(1)}, u32[]{:S(2)}, u32[]{:S(2)}) %collective-permute-start.3) | collective-permute-done | bytes 131104 | tf_op jit(solution)/shard_map/ppermute | solution.py:29
  33.5 2.3 %collective-permute-done.2.refs_0_ = bf16[256,256]{1,0:T(8,128)(2,1)S(1)} collective-permute-done((bf16[256,256]{1,0:T(8,128)(2,1)S(1)}, bf16[256,256]{1,0:T(8,128)(2,1)S(1)}, u32[]{:S(2)}, u32[]{:S(2)}) %collective-permute-start.2) | collective-permute-done | bytes 131104 | tf_op jit(solution)/shard_map/ppermute | solution.py:23
  35.8 0.0 all-to-all-done
  35.8 4.2 %shard_map.86 = (bf16[2,896,512]{2,1,0:T(8,128)(2,1)S(1)}, bf16[2,896,512]{2,1,0:T(8,128)(2,1)S(1)}, bf16[2,896,256]{2,1,0:T(8,128)(2,1)S(1)}, bf16[256,256]{1,0...) custom-call(s32[2,6]{1,0:T(2,128)S(1)} %copy-done, ...), custom_call_target="tpu_custom_call", output_to_operand_aliasing={{2}: (2, {})} | custom-call | tf_op jit(solution)/shard_map/pallas_call | solution.py:230
  40.0 4.4 %collective-permute-start.5 = (bf16[256,256]{1,0:T(8,128)(2,1)S(1)}, bf16[256,256]{1,0:T(8,128)(2,1)S(1)}, u32[]{:S(2)}, u32[]{:S(2)}) collective-permute-start(bf16[256,256]{1,0:T(8,128)(2,1)S(1)} %get-tuple-element.27), channel_id=1, source_target_pairs={{0,248},{8,0},{16,8},{24,16},{32,24},{40,32},{48,40},{56,48},{64,5... | collective-permute-start | bytes 393224 | tf_op jit(solution)/shard_map/ppermute | solution.py:23
  44.5 0.0 collective-permute-start.6
  44.5 1.9 %collective-permute-start.7 = (bf16[256,256]{1,0:T(8,128)(2,1)S(1)}, bf16[256,256]{1,0:T(8,128)(2,1)S(1)}, u32[]{:S(2)}, u32[]{:S(2)}) collective-permute-start(bf16[256,256]{1,0:T(8,128)(2,1)S(1)} %get-tuple-element.29), channel_id=1, source_target_pairs={{0,224},{8,232},{16,240},{24,248},{32,0},{40,8},{48,16},{56,24},{6... | collective-permute-start | bytes 393224 | tf_op jit(solution)/shard_map/ppermute | solution.py:23
  46.3 1.5 %collective-permute-start.8 = (bf16[256,256]{1,0:T(8,128)(2,1)S(1)}, bf16[256,256]{1,0:T(8,128)(2,1)S(1)}, u32[]{:S(2)}, u32[]{:S(2)}) collective-permute-start(bf16[256,256]{1,0:T(8,128)(2,1)S(1)} %get-tuple-element.30), channel_id=1, source_target_pairs={{0,192},{8,200},{16,208},{24,216},{32,224},{40,232},{48,240},{56,2... | collective-permute-start | bytes 393224 | tf_op jit(solution)/shard_map/ppermute | solution.py:23
  47.9 1.3 %collective-permute-start.9 = (bf16[256,256]{1,0:T(8,128)(2,1)S(1)}, bf16[256,256]{1,0:T(8,128)(2,1)S(1)}, u32[]{:S(2)}, u32[]{:S(2)}) collective-permute-start(bf16[256,256]{1,0:T(8,128)(2,1)S(1)} %get-tuple-element.31), channel_id=1, source_target_pairs={{128,0},{136,8},{144,16},{152,24},{160,32},{168,40},{176,48},{184,... | collective-permute-start | bytes 393224 | tf_op jit(solution)/shard_map/ppermute | solution.py:29
  49.1 1.7 %shard_map.87 = (bf16[256,512]{1,0:T(8,128)(2,1)}, bf16[256,512]{1,0:T(8,128)(2,1)}, f32[256,256]{1,0:T(8,128)S(1)}) custom-call(bf16[256,1024]{1,0:T(8,128)(2,1)S(1)} %bitcast.3, bf16[2,896,512]{2,1,0:T(8,128)(2,1)S(1)} %get-tuple-element.21.probs_ref, bf16[2,896,512]{2,1,0:T(8,128)(2,1)S(1)} %get-tuple-element.22.dscores_ref, ...), custom_call_target="tpu_custom_call" | custom-call | tf_op jit(solution)/shard_map/pallas_call | solution.py:245
  50.9 0.1 collective-permute-done.5.refs_0_
  51.0 4.5 %collective-permute-done.6.refs_1_ = bf16[256,256]{1,0:T(8,128)(2,1)S(1)} collective-permute-done((bf16[256,256]{1,0:T(8,128)(2,1)S(1)}, bf16[256,256]{1,0:T(8,128)(2,1)S(1)}, u32[]{:S(2)}, u32[]{:S(2)}) %collective-permute-start.6) | collective-permute-done | bytes 131104 | tf_op jit(solution)/shard_map/ppermute | solution.py:23
  55.5 1.7 %collective-permute-done.7.refs_2_ = bf16[256,256]{1,0:T(8,128)(2,1)S(1)} collective-permute-done((bf16[256,256]{1,0:T(8,128)(2,1)S(1)}, bf16[256,256]{1,0:T(8,128)(2,1)S(1)}, u32[]{:S(2)}, u32[]{:S(2)}) %collective-permute-start.7) | collective-permute-done | bytes 131104 | tf_op jit(solution)/shard_map/ppermute | solution.py:23
  57.2 0.0 collective-permute-done.8.refs_3_
  57.2 0.0 collective-permute-done.9.refs_4_
  57.2 0.7 %shard_map.88 = (bf16[256,128]{1,0:T(8,128)(2,1)}, bf16[256,128]{1,0:T(8,128)(2,1)}) custom-call(f32[256,256]{1,0:T(8,128)S(1)} %get-tuple-element.26.own_ref, bf16[256,256]{1,0:T(8,128)(2,1)S(1)} %collective-permute-done.5.refs_0_, bf16[256,256]{1,0:T(8,128)(2,1)S(1)} %collective-permute-done.6.refs_1_, ...), custom_call_target="tpu_custom_call" | custom-call | tf_op jit(solution)/shard_map/pallas_call | solution.py:254
Async XLA Ops:
  0.6 31.2 %copy-start = (s32[2,6]{1,0:T(2,128)S(1)}, s32[2,6]{1,0:T(2,128)}, u32[]{:S(2)}) copy-start(s32[2,6]{1,0:T(2,128)} %partners_ref.3) | copy-start | bytes 148
  12.4 18.3 %collective-permute-start.1 = (bf16[256,256]{1,0:T(8,128)(2,1)S(1)}, bf16[256,256]{1,0:T(8,128)(2,1)S(1)}, u32[]{:S(2)}, u32[]{:S(2)}) collective-permute-start(bf16[256,256]{1,0:T(8,128)(2,1)S(1)} %bitcast.4), channel_id=1, source_target_pairs={{0,8},{8,16},{16,24},{24,32},{32,40},{40,48},{48,56},{56,64},{64,7... | collective-permute-start | bytes 393224 | tf_op jit(solution)/shard_map/ppermute | solution.py:23
  14.4 17.5 %collective-permute-start = (bf16[256,256]{1,0:T(8,128)(2,1)S(1)}, bf16[256,256]{1,0:T(8,128)(2,1)S(1)}, u32[]{:S(2)}, u32[]{:S(2)}) collective-permute-start(bf16[256,256]{1,0:T(8,128)(2,1)S(1)} %bitcast.5), channel_id=1, source_target_pairs={{0,32},{8,40},{16,48},{24,56},{32,64},{40,72},{48,80},{56,88},{64,... | collective-permute-start | bytes 393224 | tf_op jit(solution)/shard_map/ppermute | solution.py:23
  19.8 16.1 %all-to-all-start = ((bf16[8,32,1024]{2,1,0:T(8,128)(2,1)}), bf16[8,32,1024]{2,1,0:T(8,128)(2,1)S(1)}, u32[]{:S(2)}, u32[]{:S(2)}) async-start(bf16[8,32,1024]{2,1,0:T(8,128)(2,1)} %get-tuple-element.19), calls=%async_computation | async-start | bytes 1048576 | tf_op jit(solution)/shard_map/all_to_all | solution.py:209
  24.6 7.8 %collective-permute-start.4 = (bf16[256,256]{1,0:T(8,128)(2,1)S(1)}, bf16[256,256]{1,0:T(8,128)(2,1)S(1)}, u32[]{:S(2)}, u32[]{:S(2)}) collective-permute-start(bf16[256,256]{1,0:T(8,128)(2,1)S(1)} %bitcast.6), channel_id=1, source_target_pairs={{0,64},{8,72},{16,80},{24,88},{32,96},{40,104},{48,112},{56,120},{... | collective-permute-start | bytes 393224 | tf_op jit(solution)/shard_map/ppermute | solution.py:23
  26.1 7.4 %collective-permute-start.3 = (bf16[256,256]{1,0:T(8,128)(2,1)S(1)}, bf16[256,256]{1,0:T(8,128)(2,1)S(1)}, u32[]{:S(2)}, u32[]{:S(2)}) collective-permute-start(bf16[256,256]{1,0:T(8,128)(2,1)S(1)} %bitcast.7), channel_id=1, source_target_pairs={{0,128},{8,136},{16,144},{24,152},{32,160},{40,168},{48,176},{56,1... | collective-permute-start | bytes 393224 | tf_op jit(solution)/shard_map/ppermute | solution.py:29
  30.8 5.1 %collective-permute-start.2 = (bf16[256,256]{1,0:T(8,128)(2,1)S(1)}, bf16[256,256]{1,0:T(8,128)(2,1)S(1)}, u32[]{:S(2)}, u32[]{:S(2)}) collective-permute-start(bf16[256,256]{1,0:T(8,128)(2,1)S(1)} %collective-permute-done.1.refs_1_), channel_id=1, source_target_pairs={{0,8},{8,16},{16,24},{24,32},{32,40},{40,48},{48,56},{56,64},{64,7... | collective-permute-start | bytes 393224 | tf_op jit(solution)/shard_map/ppermute | solution.py:23
  40.0 10.9 %collective-permute-start.5 = (bf16[256,256]{1,0:T(8,128)(2,1)S(1)}, bf16[256,256]{1,0:T(8,128)(2,1)S(1)}, u32[]{:S(2)}, u32[]{:S(2)}) collective-permute-start(bf16[256,256]{1,0:T(8,128)(2,1)S(1)} %get-tuple-element.27), channel_id=1, source_target_pairs={{0,248},{8,0},{16,8},{24,16},{32,24},{40,32},{48,40},{56,48},{64,5... | collective-permute-start | bytes 393224 | tf_op jit(solution)/shard_map/ppermute | solution.py:23
  44.5 11.0 %collective-permute-start.6 = (bf16[256,256]{1,0:T(8,128)(2,1)S(1)}, bf16[256,256]{1,0:T(8,128)(2,1)S(1)}, u32[]{:S(2)}, u32[]{:S(2)}) collective-permute-start(bf16[256,256]{1,0:T(8,128)(2,1)S(1)} %get-tuple-element.28), channel_id=1, source_target_pairs={{0,240},{8,248},{16,0},{24,8},{32,16},{40,24},{48,32},{56,40},{64,... | collective-permute-start | bytes 393224 | tf_op jit(solution)/shard_map/ppermute | solution.py:23
  44.5 12.7 %collective-permute-start.7 = (bf16[256,256]{1,0:T(8,128)(2,1)S(1)}, bf16[256,256]{1,0:T(8,128)(2,1)S(1)}, u32[]{:S(2)}, u32[]{:S(2)}) collective-permute-start(bf16[256,256]{1,0:T(8,128)(2,1)S(1)} %get-tuple-element.29), channel_id=1, source_target_pairs={{0,224},{8,232},{16,240},{24,248},{32,0},{40,8},{48,16},{56,24},{6... | collective-permute-start | bytes 393224 | tf_op jit(solution)/shard_map/ppermute | solution.py:23
  46.3 10.9 %collective-permute-start.8 = (bf16[256,256]{1,0:T(8,128)(2,1)S(1)}, bf16[256,256]{1,0:T(8,128)(2,1)S(1)}, u32[]{:S(2)}, u32[]{:S(2)}) collective-permute-start(bf16[256,256]{1,0:T(8,128)(2,1)S(1)} %get-tuple-element.30), channel_id=1, source_target_pairs={{0,192},{8,200},{16,208},{24,216},{32,224},{40,232},{48,240},{56,2... | collective-permute-start | bytes 393224 | tf_op jit(solution)/shard_map/ppermute | solution.py:23
  47.9 9.3 %collective-permute-start.9 = (bf16[256,256]{1,0:T(8,128)(2,1)S(1)}, bf16[256,256]{1,0:T(8,128)(2,1)S(1)}, u32[]{:S(2)}, u32[]{:S(2)}) collective-permute-start(bf16[256,256]{1,0:T(8,128)(2,1)S(1)} %get-tuple-element.31), channel_id=1, source_target_pairs={{128,0},{136,8},{144,16},{152,24},{160,32},{168,40},{176,48},{184,... | collective-permute-start | bytes 393224 | tf_op jit(solution)/shard_map/ppermute | solution.py:29

commit v4 on v3

--- a/solution.py
+++ b/solution.py
@@ -241,7 +241,7 @@
         scratch_shapes=[pltpu.VMEM((blocks, keys, 2 * HEAD_SIZE), jnp.float32)],
         compiler_params=pltpu.CompilerParams(vmem_limit_bytes=32 << 20),
     )(partners, qd, listed, *[fars[j] for j in late])
-    received = [(line if j in (4,) else ring)(part, "seq", -(2**j)) for j, part in enumerate(parts)]
+    received = [ring(part, "seq", -(2**j)) for j, part in enumerate(parts)]
     attention, grad_query, own = pl.pallas_call(
         functools.partial(outputs_kernel, q_heads),
         out_shape=[jax.ShapeDtypeStruct((tokens, q_heads * HEAD_SIZE), jnp.bfloat16)] * 2

time: 58.5 us -> 58.5 us (level)
    ppermute x8 -> x9, starting transfers between devices: 17.7 us -> 19.6 us  [ring(): lax.ppermute(value, axis, [(s, (s + steps) % count) for s in range(count)])]
    ppermute x2 -> x1, starting transfers between devices: 5.91 us -> 4.63 us  [line(): return lax.ppermute(value, axis, pairs)]
    ppermute x8 -> x9, waiting for transfers between devices: 8.62 us -> 8.06 us  [ring(): lax.ppermute(value, axis, [(s, (s + steps) % count) for s in range(count)])]
  transfers between devices with their start and end apart: 11 -> 11, of which waited for: 5 -> 4; matrix products, arithmetic and copies ran while one was open for 0% -> 0% of each run, Pallas kernels for 4% -> 4%
where the time goes in v4:
time: 58.5 us; the launch traced here: 57.9 us
  starting transfers between devices  29 us (50%)
  blocking collectives  9.6 us (16%)
  Pallas kernels  9.44 us (16%)
  waiting for transfers between devices  9.11 us (16%)
  between operations  0.7 us (1%)
    ppermute x9, starting transfers between devices, ring(): lax.ppermute(value, axis, [(s, (s + steps) % count) for s in range(count)])  19.6 us
    all_to_all x1, blocking collectives, shards(): kv = lax.all_to_all(kv, 'head', 0, 0, tiled=True)  9.6 us
    ppermute x9, waiting for transfers between devices, ring(): lax.ppermute(value, axis, [(s, (s + steps) % count) for s in range(count)])  8.06 us
    all_to_all x1, starting transfers between devices, shards(): qd = lax.all_to_all(qd, 'head', 0, 0, tiled=True)  4.86 us
    ppermute x1, starting transfers between devices, line(): return lax.ppermute(value, axis, pairs)  4.63 us
    pallas_call x1, Pallas kernels, shards(): pl.pallas_call(functools.partial(main_kernel, far_count, q_heads, late),...  4.21 us
    pallas_call x1, Pallas kernels, pack(): pl.pallas_call(pack_kernel, out_shape=[jax.ShapeDtypeStruct(shape, dtype)...  2.2 us
    pallas_call x1, Pallas kernels, shards(): pl.pallas_call(functools.partial(outputs_kernel, q_heads), out_shape=[jax...  1.72 us
  transfers between devices with their start and end apart: 11, of which 4 were waited for; matrix products, arithmetic and copies ran while one was open for 0% of the time, Pallas kernels for 4%

profile of v4, /device:TPU:40, one launch (start us, length us, event | category | flops | bytes accessed | tf_op | source)
XLA Modules:
  0.0 57.9 jit_solution(2040135973830054152)
XLA Ops:
  0.6 0.0 copy-start
  0.6 2.2 %shard_map.84 = (bf16[8,32,256]{2,1,0:T(8,128)(2,1)}, bf16[8,32,1024]{2,1,0:T(8,128)(2,1)}) custom-call(bf16[32,1024]{1,0:T(8,128)(2,1)} %refs_0_.1, bf16[32,1024]{1,0:T(8,128)(2,1)} %refs_1_.1, bf16[32,4096]{1,0:T(8,128)(2,1)} %refs_2_.1, bf16[32,4096]{1,0:T(8,128)(2,1)} %refs_3_.1), custom_call_target="tpu_custom_call" | custom-call | tf_op jit(solution)/shard_map/pallas_call | solution.py:65
  2.8 9.6 %all_to_all.10 = bf16[8,32,256]{2,1,0:T(8,128)(2,1)S(1)} all-to-all(bf16[8,32,256]{2,1,0:T(8,128)(2,1)} %get-tuple-element.20), channel_id=1, replica_groups=mesh['seq'=32,'head'=8] {'head'}, dimensions={0} | all-to-all | bytes 262144 | tf_op jit(solution)/shard_map/all_to_all | solution.py:208
  12.4 1.9 %collective-permute-start.1 = (bf16[256,256]{1,0:T(8,128)(2,1)S(1)}, bf16[256,256]{1,0:T(8,128)(2,1)S(1)}, u32[]{:S(2)}, u32[]{:S(2)}) collective-permute-start(bf16[256,256]{1,0:T(8,128)(2,1)S(1)} %bitcast.4), channel_id=1, source_target_pairs={{0,8},{8,16},{16,24},{24,32},{32,40},{40,48},{48,56},{56,64},{64,7... | collective-permute-start | bytes 393224 | tf_op jit(solution)/shard_map/ppermute | solution.py:23
  14.4 5.4 %collective-permute-start = (bf16[256,256]{1,0:T(8,128)(2,1)S(1)}, bf16[256,256]{1,0:T(8,128)(2,1)S(1)}, u32[]{:S(2)}, u32[]{:S(2)}) collective-permute-start(bf16[256,256]{1,0:T(8,128)(2,1)S(1)} %bitcast.5), channel_id=1, source_target_pairs={{0,32},{8,40},{16,48},{24,56},{32,64},{40,72},{48,80},{56,88},{64,... | collective-permute-start | bytes 393224 | tf_op jit(solution)/shard_map/ppermute | solution.py:23
  19.8 4.9 %all-to-all-start = ((bf16[8,32,1024]{2,1,0:T(8,128)(2,1)}), bf16[8,32,1024]{2,1,0:T(8,128)(2,1)S(1)}, u32[]{:S(2)}, u32[]{:S(2)}) async-start(bf16[8,32,1024]{2,1,0:T(8,128)(2,1)} %get-tuple-element.19), calls=%async_computation | async-start | bytes 1048576 | tf_op jit(solution)/shard_map/all_to_all | solution.py:209
  24.6 1.5 %collective-permute-start.4 = (bf16[256,256]{1,0:T(8,128)(2,1)S(1)}, bf16[256,256]{1,0:T(8,128)(2,1)S(1)}, u32[]{:S(2)}, u32[]{:S(2)}) collective-permute-start(bf16[256,256]{1,0:T(8,128)(2,1)S(1)} %bitcast.6), channel_id=1, source_target_pairs={{0,64},{8,72},{16,80},{24,88},{32,96},{40,104},{48,112},{56,120},{... | collective-permute-start | bytes 393224 | tf_op jit(solution)/shard_map/ppermute | solution.py:23
  26.1 4.6 %collective-permute-start.3 = (bf16[256,256]{1,0:T(8,128)(2,1)S(1)}, bf16[256,256]{1,0:T(8,128)(2,1)S(1)}, u32[]{:S(2)}, u32[]{:S(2)}) collective-permute-start(bf16[256,256]{1,0:T(8,128)(2,1)S(1)} %bitcast.7), channel_id=1, source_target_pairs={{0,128},{8,136},{16,144},{24,152},{32,160},{40,168},{48,176},{56,1... | collective-permute-start | bytes 393224 | tf_op jit(solution)/shard_map/ppermute | solution.py:29
  30.7 0.0 collective-permute-done.1.refs_1_
  30.8 1.1 %collective-permute-start.2 = (bf16[256,256]{1,0:T(8,128)(2,1)S(1)}, bf16[256,256]{1,0:T(8,128)(2,1)S(1)}, u32[]{:S(2)}, u32[]{:S(2)}) collective-permute-start(bf16[256,256]{1,0:T(8,128)(2,1)S(1)} %collective-permute-done.1.refs_1_), channel_id=1, source_target_pairs={{0,8},{8,16},{16,24},{24,32},{32,40},{40,48},{48,56},{56,64},{64,7... | collective-permute-start | bytes 393224 | tf_op jit(solution)/shard_map/ppermute | solution.py:23
  31.9 0.0 collective-permute-done.refs_0_
  31.9 0.0 copy-done
  31.9 0.6 %shard_map.85.listed_ref = bf16[2,896,256]{2,1,0:T(8,128)(2,1)S(1)} custom-call(s32[2,6]{1,0:T(2,128)S(1)} %copy-done, bf16[256,256]{1,0:T(8,128)(2,1)S(1)} %bitcast.8, bf16[256,256]{1,0:T(8,128)(2,1)S(1)} %collective-permute-done.refs_0_, bf16[256,256]{1,0:T(8,128)(2,1)S(1)} %collective-permute-done.1.refs_1_), custom_call_target="tpu_custom_call" | custom-call | flops 10000000000 | tf_op jit(solution)/shard_map/pallas_call | solution.py:222
  32.5 0.0 collective-permute-done.4.refs_2_
  32.5 1.0 %collective-permute-done.3.refs_1_ = bf16[256,256]{1,0:T(8,128)(2,1)S(1)} collective-permute-done((bf16[256,256]{1,0:T(8,128)(2,1)S(1)}, bf16[256,256]{1,0:T(8,128)(2,1)S(1)}, u32[]{:S(2)}, u32[]{:S(2)}) %collective-permute-start.3) | collective-permute-done | bytes 131104 | tf_op jit(solution)/shard_map/ppermute | solution.py:29
  33.5 2.3 %collective-permute-done.2.refs_0_ = bf16[256,256]{1,0:T(8,128)(2,1)S(1)} collective-permute-done((bf16[256,256]{1,0:T(8,128)(2,1)S(1)}, bf16[256,256]{1,0:T(8,128)(2,1)S(1)}, u32[]{:S(2)}, u32[]{:S(2)}) %collective-permute-start.2) | collective-permute-done | bytes 131104 | tf_op jit(solution)/shard_map/ppermute | solution.py:23
  35.8 0.0 all-to-all-done
  35.8 4.2 %shard_map.86 = (bf16[2,896,512]{2,1,0:T(8,128)(2,1)S(1)}, bf16[2,896,512]{2,1,0:T(8,128)(2,1)S(1)}, bf16[2,896,256]{2,1,0:T(8,128)(2,1)S(1)}, bf16[256,256]{1,0...) custom-call(s32[2,6]{1,0:T(2,128)S(1)} %copy-done, ...), custom_call_target="tpu_custom_call", output_to_operand_aliasing={{2}: (2, {})} | custom-call | tf_op jit(solution)/shard_map/pallas_call | solution.py:230
  40.0 4.4 %collective-permute-start.5 = (bf16[256,256]{1,0:T(8,128)(2,1)S(1)}, bf16[256,256]{1,0:T(8,128)(2,1)S(1)}, u32[]{:S(2)}, u32[]{:S(2)}) collective-permute-start(bf16[256,256]{1,0:T(8,128)(2,1)S(1)} %get-tuple-element.27), channel_id=1, source_target_pairs={{0,248},{8,0},{16,8},{24,16},{32,24},{40,32},{48,40},{56,48},{64,5... | collective-permute-start | bytes 393224 | tf_op jit(solution)/shard_map/ppermute | solution.py:23
  44.5 0.0 collective-permute-start.6
  44.5 1.9 %collective-permute-start.7 = (bf16[256,256]{1,0:T(8,128)(2,1)S(1)}, bf16[256,256]{1,0:T(8,128)(2,1)S(1)}, u32[]{:S(2)}, u32[]{:S(2)}) collective-permute-start(bf16[256,256]{1,0:T(8,128)(2,1)S(1)} %get-tuple-element.29), channel_id=1, source_target_pairs={{0,224},{8,232},{16,240},{24,248},{32,0},{40,8},{48,16},{56,24},{6... | collective-permute-start | bytes 393224 | tf_op jit(solution)/shard_map/ppermute | solution.py:23
  46.3 1.5 %collective-permute-start.8 = (bf16[256,256]{1,0:T(8,128)(2,1)S(1)}, bf16[256,256]{1,0:T(8,128)(2,1)S(1)}, u32[]{:S(2)}, u32[]{:S(2)}) collective-permute-start(bf16[256,256]{1,0:T(8,128)(2,1)S(1)} %get-tuple-element.30), channel_id=1, source_target_pairs={{0,192},{8,200},{16,208},{24,216},{32,224},{40,232},{48,240},{56,2... | collective-permute-start | bytes 393224 | tf_op jit(solution)/shard_map/ppermute | solution.py:23
  47.9 1.9 %collective-permute-start.9 = (bf16[256,256]{1,0:T(8,128)(2,1)S(1)}, bf16[256,256]{1,0:T(8,128)(2,1)S(1)}, u32[]{:S(2)}, u32[]{:S(2)}) collective-permute-start(bf16[256,256]{1,0:T(8,128)(2,1)S(1)} %get-tuple-element.31), channel_id=1, source_target_pairs={{0,128},{8,136},{16,144},{24,152},{32,160},{40,168},{48,176},{56,1... | collective-permute-start | bytes 393224 | tf_op jit(solution)/shard_map/ppermute | solution.py:23
  49.7 1.7 %shard_map.87 = (bf16[256,512]{1,0:T(8,128)(2,1)}, bf16[256,512]{1,0:T(8,128)(2,1)}, f32[256,256]{1,0:T(8,128)S(1)}) custom-call(bf16[256,1024]{1,0:T(8,128)(2,1)S(1)} %bitcast.3, bf16[2,896,512]{2,1,0:T(8,128)(2,1)S(1)} %get-tuple-element.21.probs_ref, bf16[2,896,512]{2,1,0:T(8,128)(2,1)S(1)} %get-tuple-element.22.dscores_ref, ...), custom_call_target="tpu_custom_call" | custom-call | tf_op jit(solution)/shard_map/pallas_call | solution.py:245
  51.4 0.0 collective-permute-done.5.refs_0_
  51.4 4.0 %collective-permute-done.6.refs_1_ = bf16[256,256]{1,0:T(8,128)(2,1)S(1)} collective-permute-done((bf16[256,256]{1,0:T(8,128)(2,1)S(1)}, bf16[256,256]{1,0:T(8,128)(2,1)S(1)}, u32[]{:S(2)}, u32[]{:S(2)}) %collective-permute-start.6) | collective-permute-done | bytes 131104 | tf_op jit(solution)/shard_map/ppermute | solution.py:23
  55.5 1.7 %collective-permute-done.7.refs_2_ = bf16[256,256]{1,0:T(8,128)(2,1)S(1)} collective-permute-done((bf16[256,256]{1,0:T(8,128)(2,1)S(1)}, bf16[256,256]{1,0:T(8,128)(2,1)S(1)}, u32[]{:S(2)}, u32[]{:S(2)}) %collective-permute-start.7) | collective-permute-done | bytes 131104 | tf_op jit(solution)/shard_map/ppermute | solution.py:23
  57.2 0.0 collective-permute-done.8.refs_3_
  57.2 0.0 collective-permute-done.9.refs_4_
  57.2 0.7 %shard_map.88 = (bf16[256,128]{1,0:T(8,128)(2,1)}, bf16[256,128]{1,0:T(8,128)(2,1)}) custom-call(f32[256,256]{1,0:T(8,128)S(1)} %get-tuple-element.26.own_ref, bf16[256,256]{1,0:T(8,128)(2,1)S(1)} %collective-permute-done.5.refs_0_, bf16[256,256]{1,0:T(8,128)(2,1)S(1)} %collective-permute-done.6.refs_1_, ...), custom_call_target="tpu_custom_call" | custom-call | tf_op jit(solution)/shard_map/pallas_call | solution.py:254
Async XLA Ops:
  0.6 31.2 %copy-start = (s32[2,6]{1,0:T(2,128)S(1)}, s32[2,6]{1,0:T(2,128)}, u32[]{:S(2)}) copy-start(s32[2,6]{1,0:T(2,128)} %partners_ref.3) | copy-start | bytes 148
  12.4 18.3 %collective-permute-start.1 = (bf16[256,256]{1,0:T(8,128)(2,1)S(1)}, bf16[256,256]{1,0:T(8,128)(2,1)S(1)}, u32[]{:S(2)}, u32[]{:S(2)}) collective-permute-start(bf16[256,256]{1,0:T(8,128)(2,1)S(1)} %bitcast.4), channel_id=1, source_target_pairs={{0,8},{8,16},{16,24},{24,32},{32,40},{40,48},{48,56},{56,64},{64,7... | collective-permute-start | bytes 393224 | tf_op jit(solution)/shard_map/ppermute | solution.py:23
  14.4 17.5 %collective-permute-start = (bf16[256,256]{1,0:T(8,128)(2,1)S(1)}, bf16[256,256]{1,0:T(8,128)(2,1)S(1)}, u32[]{:S(2)}, u32[]{:S(2)}) collective-permute-start(bf16[256,256]{1,0:T(8,128)(2,1)S(1)} %bitcast.5), channel_id=1, source_target_pairs={{0,32},{8,40},{16,48},{24,56},{32,64},{40,72},{48,80},{56,88},{64,... | collective-permute-start | bytes 393224 | tf_op jit(solution)/shard_map/ppermute | solution.py:23
  19.8 16.1 %all-to-all-start = ((bf16[8,32,1024]{2,1,0:T(8,128)(2,1)}), bf16[8,32,1024]{2,1,0:T(8,128)(2,1)S(1)}, u32[]{:S(2)}, u32[]{:S(2)}) async-start(bf16[8,32,1024]{2,1,0:T(8,128)(2,1)} %get-tuple-element.19), calls=%async_computation | async-start | bytes 1048576 | tf_op jit(solution)/shard_map/all_to_all | solution.py:209
  24.6 7.8 %collective-permute-start.4 = (bf16[256,256]{1,0:T(8,128)(2,1)S(1)}, bf16[256,256]{1,0:T(8,128)(2,1)S(1)}, u32[]{:S(2)}, u32[]{:S(2)}) collective-permute-start(bf16[256,256]{1,0:T(8,128)(2,1)S(1)} %bitcast.6), channel_id=1, source_target_pairs={{0,64},{8,72},{16,80},{24,88},{32,96},{40,104},{48,112},{56,120},{... | collective-permute-start | bytes 393224 | tf_op jit(solution)/shard_map/ppermute | solution.py:23
  26.1 7.4 %collective-permute-start.3 = (bf16[256,256]{1,0:T(8,128)(2,1)S(1)}, bf16[256,256]{1,0:T(8,128)(2,1)S(1)}, u32[]{:S(2)}, u32[]{:S(2)}) collective-permute-start(bf16[256,256]{1,0:T(8,128)(2,1)S(1)} %bitcast.7), channel_id=1, source_target_pairs={{0,128},{8,136},{16,144},{24,152},{32,160},{40,168},{48,176},{56,1... | collective-permute-start | bytes 393224 | tf_op jit(solution)/shard_map/ppermute | solution.py:29
  30.8 5.1 %collective-permute-start.2 = (bf16[256,256]{1,0:T(8,128)(2,1)S(1)}, bf16[256,256]{1,0:T(8,128)(2,1)S(1)}, u32[]{:S(2)}, u32[]{:S(2)}) collective-permute-start(bf16[256,256]{1,0:T(8,128)(2,1)S(1)} %collective-permute-done.1.refs_1_), channel_id=1, source_target_pairs={{0,8},{8,16},{16,24},{24,32},{32,40},{40,48},{48,56},{56,64},{64,7... | collective-permute-start | bytes 393224 | tf_op jit(solution)/shard_map/ppermute | solution.py:23
  40.0 11.4 %collective-permute-start.5 = (bf16[256,256]{1,0:T(8,128)(2,1)S(1)}, bf16[256,256]{1,0:T(8,128)(2,1)S(1)}, u32[]{:S(2)}, u32[]{:S(2)}) collective-permute-start(bf16[256,256]{1,0:T(8,128)(2,1)S(1)} %get-tuple-element.27), channel_id=1, source_target_pairs={{0,248},{8,0},{16,8},{24,16},{32,24},{40,32},{48,40},{56,48},{64,5... | collective-permute-start | bytes 393224 | tf_op jit(solution)/shard_map/ppermute | solution.py:23
  44.5 11.0 %collective-permute-start.6 = (bf16[256,256]{1,0:T(8,128)(2,1)S(1)}, bf16[256,256]{1,0:T(8,128)(2,1)S(1)}, u32[]{:S(2)}, u32[]{:S(2)}) collective-permute-start(bf16[256,256]{1,0:T(8,128)(2,1)S(1)} %get-tuple-element.28), channel_id=1, source_target_pairs={{0,240},{8,248},{16,0},{24,8},{32,16},{40,24},{48,32},{56,40},{64,... | collective-permute-start | bytes 393224 | tf_op jit(solution)/shard_map/ppermute | solution.py:23
  44.5 12.7 %collective-permute-start.7 = (bf16[256,256]{1,0:T(8,128)(2,1)S(1)}, bf16[256,256]{1,0:T(8,128)(2,1)S(1)}, u32[]{:S(2)}, u32[]{:S(2)}) collective-permute-start(bf16[256,256]{1,0:T(8,128)(2,1)S(1)} %get-tuple-element.29), channel_id=1, source_target_pairs={{0,224},{8,232},{16,240},{24,248},{32,0},{40,8},{48,16},{56,24},{6... | collective-permute-start | bytes 393224 | tf_op jit(solution)/shard_map/ppermute | solution.py:23
  46.3 10.9 %collective-permute-start.8 = (bf16[256,256]{1,0:T(8,128)(2,1)S(1)}, bf16[256,256]{1,0:T(8,128)(2,1)S(1)}, u32[]{:S(2)}, u32[]{:S(2)}) collective-permute-start(bf16[256,256]{1,0:T(8,128)(2,1)S(1)} %get-tuple-element.30), channel_id=1, source_target_pairs={{0,192},{8,200},{16,208},{24,216},{32,224},{40,232},{48,240},{56,2... | collective-permute-start | bytes 393224 | tf_op jit(solution)/shard_map/ppermute | solution.py:23
  47.9 9.3 %collective-permute-start.9 = (bf16[256,256]{1,0:T(8,128)(2,1)S(1)}, bf16[256,256]{1,0:T(8,128)(2,1)S(1)}, u32[]{:S(2)}, u32[]{:S(2)}) collective-permute-start(bf16[256,256]{1,0:T(8,128)(2,1)S(1)} %get-tuple-element.31), channel_id=1, source_target_pairs={{0,128},{8,136},{16,144},{24,152},{32,160},{40,168},{48,176},{56,1... | collective-permute-start | bytes 393224 | tf_op jit(solution)/shard_map/ppermute | solution.py:23

commit v5 on v4

--- a/solution.py
+++ b/solution.py
@@ -122,7 +122,7 @@
     slots = 2 + far_count
     size = BLOCK_TOKENS
     q_columns = q_heads * HEAD_SIZE
-    pair = 2
+    pair = 4
     fill(cat_ref, partners_ref, dict(zip(late, far_refs, strict=True)))
 
     causal = lax.broadcasted_iota(jnp.int32, (size, size), 0) <= lax.broadcasted_iota(jnp.int32, (size, size), 1)
@@ -215,7 +215,7 @@
     far_count = partners.shape[1] - 1
     fars = {j: (line if j in (4,) else ring)(kv, "seq", 2**j) for j in range(far_count) if j != 1}
     fars[1] = ring(fars[0], "seq", 1)
-    late = (1, 4, 3)
+    late = (4, 3, 1)
     keys = (2 + far_count) * BLOCK_TOKENS
     big = (blocks, keys, q_heads * BLOCK_TOKENS)
     cat_type = jax.ShapeDtypeStruct((blocks, keys, 2 * HEAD_SIZE), jnp.bfloat16)

time: 58.5 us -> 58.5 us (level)
  no operation moved by 1% of the time
where the time goes in v5:
time: 58.5 us; the launch traced here: 57.8 us
  starting transfers between devices  29 us (50%)
  blocking collectives  9.6 us (16%)
  Pallas kernels  9.38 us (16%)
  waiting for transfers between devices  9.09 us (16%)
  between operations  0.7 us (1%)
    ppermute x9, starting transfers between devices, ring(): lax.ppermute(value, axis, [(s, (s + steps) % count) for s in range(count)])  19.6 us
    all_to_all x1, blocking collectives, shards(): kv = lax.all_to_all(kv, 'head', 0, 0, tiled=True)  9.6 us
    ppermute x9, waiting for transfers between devices, ring(): lax.ppermute(value, axis, [(s, (s + steps) % count) for s in range(count)])  8.04 us
    all_to_all x1, starting transfers between devices, shards(): qd = lax.all_to_all(qd, 'head', 0, 0, tiled=True)  4.86 us
    ppermute x1, starting transfers between devices, line(): return lax.ppermute(value, axis, pairs)  4.63 us
    pallas_call x1, Pallas kernels, shards(): pl.pallas_call(functools.partial(main_kernel, far_count, q_heads, late),...  4.14 us
    pallas_call x1, Pallas kernels, pack(): pl.pallas_call(pack_kernel, out_shape=[jax.ShapeDtypeStruct(shape, dtype)...  2.2 us
    pallas_call x1, Pallas kernels, shards(): pl.pallas_call(functools.partial(outputs_kernel, q_heads), out_shape=[jax...  1.73 us
  transfers between devices with their start and end apart: 11, of which 4 were waited for; matrix products, arithmetic and copies ran while one was open for 0% of the time, Pallas kernels for 4%

profile of v5, /device:TPU:40, one launch (start us, length us, event | category | flops | bytes accessed | tf_op | source)
XLA Modules:
  0.0 57.8 jit_solution(10830583626516386035)
XLA Ops:
  0.6 0.0 copy-start
  0.6 2.2 %shard_map.84 = (bf16[8,32,256]{2,1,0:T(8,128)(2,1)}, bf16[8,32,1024]{2,1,0:T(8,128)(2,1)}) custom-call(bf16[32,1024]{1,0:T(8,128)(2,1)} %refs_0_.1, bf16[32,1024]{1,0:T(8,128)(2,1)} %refs_1_.1, bf16[32,4096]{1,0:T(8,128)(2,1)} %refs_2_.1, bf16[32,4096]{1,0:T(8,128)(2,1)} %refs_3_.1), custom_call_target="tpu_custom_call" | custom-call | tf_op jit(solution)/shard_map/pallas_call | solution.py:65
  2.8 9.6 %all_to_all.10 = bf16[8,32,256]{2,1,0:T(8,128)(2,1)S(1)} all-to-all(bf16[8,32,256]{2,1,0:T(8,128)(2,1)} %get-tuple-element.20), channel_id=1, replica_groups=mesh['seq'=32,'head'=8] {'head'}, dimensions={0} | all-to-all | bytes 262144 | tf_op jit(solution)/shard_map/all_to_all | solution.py:208
  12.4 1.9 %collective-permute-start.1 = (bf16[256,256]{1,0:T(8,128)(2,1)S(1)}, bf16[256,256]{1,0:T(8,128)(2,1)S(1)}, u32[]{:S(2)}, u32[]{:S(2)}) collective-permute-start(bf16[256,256]{1,0:T(8,128)(2,1)S(1)} %bitcast.4), channel_id=1, source_target_pairs={{0,8},{8,16},{16,24},{24,32},{32,40},{40,48},{48,56},{56,64},{64,7... | collective-permute-start | bytes 393224 | tf_op jit(solution)/shard_map/ppermute | solution.py:23
  14.4 5.4 %collective-permute-start = (bf16[256,256]{1,0:T(8,128)(2,1)S(1)}, bf16[256,256]{1,0:T(8,128)(2,1)S(1)}, u32[]{:S(2)}, u32[]{:S(2)}) collective-permute-start(bf16[256,256]{1,0:T(8,128)(2,1)S(1)} %bitcast.5), channel_id=1, source_target_pairs={{0,32},{8,40},{16,48},{24,56},{32,64},{40,72},{48,80},{56,88},{64,... | collective-permute-start | bytes 393224 | tf_op jit(solution)/shard_map/ppermute | solution.py:23
  19.8 4.9 %all-to-all-start = ((bf16[8,32,1024]{2,1,0:T(8,128)(2,1)}), bf16[8,32,1024]{2,1,0:T(8,128)(2,1)S(1)}, u32[]{:S(2)}, u32[]{:S(2)}) async-start(bf16[8,32,1024]{2,1,0:T(8,128)(2,1)} %get-tuple-element.19), calls=%async_computation | async-start | bytes 1048576 | tf_op jit(solution)/shard_map/all_to_all | solution.py:209
  24.6 1.5 %collective-permute-start.3 = (bf16[256,256]{1,0:T(8,128)(2,1)S(1)}, bf16[256,256]{1,0:T(8,128)(2,1)S(1)}, u32[]{:S(2)}, u32[]{:S(2)}) collective-permute-start(bf16[256,256]{1,0:T(8,128)(2,1)S(1)} %bitcast.6), channel_id=1, source_target_pairs={{0,64},{8,72},{16,80},{24,88},{32,96},{40,104},{48,112},{56,120},{... | collective-permute-start | bytes 393224 | tf_op jit(solution)/shard_map/ppermute | solution.py:23
  26.1 4.6 %collective-permute-start.2 = (bf16[256,256]{1,0:T(8,128)(2,1)S(1)}, bf16[256,256]{1,0:T(8,128)(2,1)S(1)}, u32[]{:S(2)}, u32[]{:S(2)}) collective-permute-start(bf16[256,256]{1,0:T(8,128)(2,1)S(1)} %bitcast.7), channel_id=1, source_target_pairs={{0,128},{8,136},{16,144},{24,152},{32,160},{40,168},{48,176},{56,1... | collective-permute-start | bytes 393224 | tf_op jit(solution)/shard_map/ppermute | solution.py:29
  30.7 0.0 collective-permute-done.1.refs_1_
  30.8 1.1 %collective-permute-start.4 = (bf16[256,256]{1,0:T(8,128)(2,1)S(1)}, bf16[256,256]{1,0:T(8,128)(2,1)S(1)}, u32[]{:S(2)}, u32[]{:S(2)}) collective-permute-start(bf16[256,256]{1,0:T(8,128)(2,1)S(1)} %collective-permute-done.1.refs_1_), channel_id=1, source_target_pairs={{0,8},{8,16},{16,24},{24,32},{32,40},{40,48},{48,56},{56,64},{64,7... | collective-permute-start | bytes 393224 | tf_op jit(solution)/shard_map/ppermute | solution.py:23
  31.9 0.0 collective-permute-done.refs_0_
  31.9 0.0 copy-done
  31.9 0.6 %shard_map.85.listed_ref = bf16[2,896,256]{2,1,0:T(8,128)(2,1)S(1)} custom-call(s32[2,6]{1,0:T(2,128)S(1)} %copy-done, bf16[256,256]{1,0:T(8,128)(2,1)S(1)} %bitcast.8, bf16[256,256]{1,0:T(8,128)(2,1)S(1)} %collective-permute-done.refs_0_, bf16[256,256]{1,0:T(8,128)(2,1)S(1)} %collective-permute-done.1.refs_1_), custom_call_target="tpu_custom_call" | custom-call | flops 10000000000 | tf_op jit(solution)/shard_map/pallas_call | solution.py:222
  32.5 0.0 collective-permute-done.3.refs_1_
  32.5 1.0 %collective-permute-done.2.refs_0_ = bf16[256,256]{1,0:T(8,128)(2,1)S(1)} collective-permute-done((bf16[256,256]{1,0:T(8,128)(2,1)S(1)}, bf16[256,256]{1,0:T(8,128)(2,1)S(1)}, u32[]{:S(2)}, u32[]{:S(2)}) %collective-permute-start.2) | collective-permute-done | bytes 131104 | tf_op jit(solution)/shard_map/ppermute | solution.py:29
  33.5 2.3 %collective-permute-done.4.refs_2_ = bf16[256,256]{1,0:T(8,128)(2,1)S(1)} collective-permute-done((bf16[256,256]{1,0:T(8,128)(2,1)S(1)}, bf16[256,256]{1,0:T(8,128)(2,1)S(1)}, u32[]{:S(2)}, u32[]{:S(2)}) %collective-permute-start.4) | collective-permute-done | bytes 131104 | tf_op jit(solution)/shard_map/ppermute | solution.py:23
  35.8 0.0 all-to-all-done
  35.8 4.1 %shard_map.86 = (bf16[2,896,512]{2,1,0:T(8,128)(2,1)S(1)}, bf16[2,896,512]{2,1,0:T(8,128)(2,1)S(1)}, bf16[2,896,256]{2,1,0:T(8,128)(2,1)S(1)}, bf16[256,256]{1,0...) custom-call(s32[2,6]{1,0:T(2,128)S(1)} %copy-done, ...), custom_call_target="tpu_custom_call", output_to_operand_aliasing={{2}: (2, {})} | custom-call | tf_op jit(solution)/shard_map/pallas_call | solution.py:230
  40.0 4.4 %collective-permute-start.5 = (bf16[256,256]{1,0:T(8,128)(2,1)S(1)}, bf16[256,256]{1,0:T(8,128)(2,1)S(1)}, u32[]{:S(2)}, u32[]{:S(2)}) collective-permute-start(bf16[256,256]{1,0:T(8,128)(2,1)S(1)} %get-tuple-element.27), channel_id=1, source_target_pairs={{0,248},{8,0},{16,8},{24,16},{32,24},{40,32},{48,40},{56,48},{64,5... | collective-permute-start | bytes 393224 | tf_op jit(solution)/shard_map/ppermute | solution.py:23
  44.4 0.0 collective-permute-start.6
  44.4 1.8 %collective-permute-start.7 = (bf16[256,256]{1,0:T(8,128)(2,1)S(1)}, bf16[256,256]{1,0:T(8,128)(2,1)S(1)}, u32[]{:S(2)}, u32[]{:S(2)}) collective-permute-start(bf16[256,256]{1,0:T(8,128)(2,1)S(1)} %get-tuple-element.29), channel_id=1, source_target_pairs={{0,224},{8,232},{16,240},{24,248},{32,0},{40,8},{48,16},{56,24},{6... | collective-permute-start | bytes 393224 | tf_op jit(solution)/shard_map/ppermute | solution.py:23
  46.2 1.5 %collective-permute-start.8 = (bf16[256,256]{1,0:T(8,128)(2,1)S(1)}, bf16[256,256]{1,0:T(8,128)(2,1)S(1)}, u32[]{:S(2)}, u32[]{:S(2)}) collective-permute-start(bf16[256,256]{1,0:T(8,128)(2,1)S(1)} %get-tuple-element.30), channel_id=1, source_target_pairs={{0,192},{8,200},{16,208},{24,216},{32,224},{40,232},{48,240},{56,2... | collective-permute-start | bytes 393224 | tf_op jit(solution)/shard_map/ppermute | solution.py:23
  47.8 1.9 %collective-permute-start.9 = (bf16[256,256]{1,0:T(8,128)(2,1)S(1)}, bf16[256,256]{1,0:T(8,128)(2,1)S(1)}, u32[]{:S(2)}, u32[]{:S(2)}) collective-permute-start(bf16[256,256]{1,0:T(8,128)(2,1)S(1)} %get-tuple-element.31), channel_id=1, source_target_pairs={{0,128},{8,136},{16,144},{24,152},{32,160},{40,168},{48,176},{56,1... | collective-permute-start | bytes 393224 | tf_op jit(solution)/shard_map/ppermute | solution.py:23
  49.6 1.7 %shard_map.87 = (bf16[256,512]{1,0:T(8,128)(2,1)}, bf16[256,512]{1,0:T(8,128)(2,1)}, f32[256,256]{1,0:T(8,128)S(1)}) custom-call(bf16[256,1024]{1,0:T(8,128)(2,1)S(1)} %bitcast.3, bf16[2,896,512]{2,1,0:T(8,128)(2,1)S(1)} %get-tuple-element.21.probs_ref, bf16[2,896,512]{2,1,0:T(8,128)(2,1)S(1)} %get-tuple-element.22.dscores_ref, ...), custom_call_target="tpu_custom_call" | custom-call | tf_op jit(solution)/shard_map/pallas_call | solution.py:245
  51.4 0.0 collective-permute-done.5.refs_0_
  51.4 4.0 %collective-permute-done.6.refs_1_ = bf16[256,256]{1,0:T(8,128)(2,1)S(1)} collective-permute-done((bf16[256,256]{1,0:T(8,128)(2,1)S(1)}, bf16[256,256]{1,0:T(8,128)(2,1)S(1)}, u32[]{:S(2)}, u32[]{:S(2)}) %collective-permute-start.6) | collective-permute-done | bytes 131104 | tf_op jit(solution)/shard_map/ppermute | solution.py:23
  55.4 1.7 %collective-permute-done.7.refs_2_ = bf16[256,256]{1,0:T(8,128)(2,1)S(1)} collective-permute-done((bf16[256,256]{1,0:T(8,128)(2,1)S(1)}, bf16[256,256]{1,0:T(8,128)(2,1)S(1)}, u32[]{:S(2)}, u32[]{:S(2)}) %collective-permute-start.7) | collective-permute-done | bytes 131104 | tf_op jit(solution)/shard_map/ppermute | solution.py:23
  57.1 0.0 collective-permute-done.8.refs_3_
  57.1 0.0 collective-permute-done.9.refs_4_
  57.1 0.7 %shard_map.88 = (bf16[256,128]{1,0:T(8,128)(2,1)}, bf16[256,128]{1,0:T(8,128)(2,1)}) custom-call(f32[256,256]{1,0:T(8,128)S(1)} %get-tuple-element.26.own_ref, bf16[256,256]{1,0:T(8,128)(2,1)S(1)} %collective-permute-done.5.refs_0_, bf16[256,256]{1,0:T(8,128)(2,1)S(1)} %collective-permute-done.6.refs_1_, ...), custom_call_target="tpu_custom_call" | custom-call | tf_op jit(solution)/shard_map/pallas_call | solution.py:254
Async XLA Ops:
  0.6 31.2 %copy-start = (s32[2,6]{1,0:T(2,128)S(1)}, s32[2,6]{1,0:T(2,128)}, u32[]{:S(2)}) copy-start(s32[2,6]{1,0:T(2,128)} %partners_ref.3) | copy-start | bytes 148
  12.4 18.3 %collective-permute-start.1 = (bf16[256,256]{1,0:T(8,128)(2,1)S(1)}, bf16[256,256]{1,0:T(8,128)(2,1)S(1)}, u32[]{:S(2)}, u32[]{:S(2)}) collective-permute-start(bf16[256,256]{1,0:T(8,128)(2,1)S(1)} %bitcast.4), channel_id=1, source_target_pairs={{0,8},{8,16},{16,24},{24,32},{32,40},{40,48},{48,56},{56,64},{64,7... | collective-permute-start | bytes 393224 | tf_op jit(solution)/shard_map/ppermute | solution.py:23
  14.4 17.5 %collective-permute-start = (bf16[256,256]{1,0:T(8,128)(2,1)S(1)}, bf16[256,256]{1,0:T(8,128)(2,1)S(1)}, u32[]{:S(2)}, u32[]{:S(2)}) collective-permute-start(bf16[256,256]{1,0:T(8,128)(2,1)S(1)} %bitcast.5), channel_id=1, source_target_pairs={{0,32},{8,40},{16,48},{24,56},{32,64},{40,72},{48,80},{56,88},{64,... | collective-permute-start | bytes 393224 | tf_op jit(solution)/shard_map/ppermute | solution.py:23
  19.8 16.1 %all-to-all-start = ((bf16[8,32,1024]{2,1,0:T(8,128)(2,1)}), bf16[8,32,1024]{2,1,0:T(8,128)(2,1)S(1)}, u32[]{:S(2)}, u32[]{:S(2)}) async-start(bf16[8,32,1024]{2,1,0:T(8,128)(2,1)} %get-tuple-element.19), calls=%async_computation | async-start | bytes 1048576 | tf_op jit(solution)/shard_map/all_to_all | solution.py:209
  24.6 7.8 %collective-permute-start.3 = (bf16[256,256]{1,0:T(8,128)(2,1)S(1)}, bf16[256,256]{1,0:T(8,128)(2,1)S(1)}, u32[]{:S(2)}, u32[]{:S(2)}) collective-permute-start(bf16[256,256]{1,0:T(8,128)(2,1)S(1)} %bitcast.6), channel_id=1, source_target_pairs={{0,64},{8,72},{16,80},{24,88},{32,96},{40,104},{48,112},{56,120},{... | collective-permute-start | bytes 393224 | tf_op jit(solution)/shard_map/ppermute | solution.py:23
  26.1 7.4 %collective-permute-start.2 = (bf16[256,256]{1,0:T(8,128)(2,1)S(1)}, bf16[256,256]{1,0:T(8,128)(2,1)S(1)}, u32[]{:S(2)}, u32[]{:S(2)}) collective-permute-start(bf16[256,256]{1,0:T(8,128)(2,1)S(1)} %bitcast.7), channel_id=1, source_target_pairs={{0,128},{8,136},{16,144},{24,152},{32,160},{40,168},{48,176},{56,1... | collective-permute-start | bytes 393224 | tf_op jit(solution)/shard_map/ppermute | solution.py:29
  30.8 5.1 %collective-permute-start.4 = (bf16[256,256]{1,0:T(8,128)(2,1)S(1)}, bf16[256,256]{1,0:T(8,128)(2,1)S(1)}, u32[]{:S(2)}, u32[]{:S(2)}) collective-permute-start(bf16[256,256]{1,0:T(8,128)(2,1)S(1)} %collective-permute-done.1.refs_1_), channel_id=1, source_target_pairs={{0,8},{8,16},{16,24},{24,32},{32,40},{40,48},{48,56},{56,64},{64,7... | collective-permute-start | bytes 393224 | tf_op jit(solution)/shard_map/ppermute | solution.py:23
  40.0 11.4 %collective-permute-start.5 = (bf16[256,256]{1,0:T(8,128)(2,1)S(1)}, bf16[256,256]{1,0:T(8,128)(2,1)S(1)}, u32[]{:S(2)}, u32[]{:S(2)}) collective-permute-start(bf16[256,256]{1,0:T(8,128)(2,1)S(1)} %get-tuple-element.27), channel_id=1, source_target_pairs={{0,248},{8,0},{16,8},{24,16},{32,24},{40,32},{48,40},{56,48},{64,5... | collective-permute-start | bytes 393224 | tf_op jit(solution)/shard_map/ppermute | solution.py:23
  44.4 11.0 %collective-permute-start.6 = (bf16[256,256]{1,0:T(8,128)(2,1)S(1)}, bf16[256,256]{1,0:T(8,128)(2,1)S(1)}, u32[]{:S(2)}, u32[]{:S(2)}) collective-permute-start(bf16[256,256]{1,0:T(8,128)(2,1)S(1)} %get-tuple-element.28), channel_id=1, source_target_pairs={{0,240},{8,248},{16,0},{24,8},{32,16},{40,24},{48,32},{56,40},{64,... | collective-permute-start | bytes 393224 | tf_op jit(solution)/shard_map/ppermute | solution.py:23
  44.4 12.7 %collective-permute-start.7 = (bf16[256,256]{1,0:T(8,128)(2,1)S(1)}, bf16[256,256]{1,0:T(8,128)(2,1)S(1)}, u32[]{:S(2)}, u32[]{:S(2)}) collective-permute-start(bf16[256,256]{1,0:T(8,128)(2,1)S(1)} %get-tuple-element.29), channel_id=1, source_target_pairs={{0,224},{8,232},{16,240},{24,248},{32,0},{40,8},{48,16},{56,24},{6... | collective-permute-start | bytes 393224 | tf_op jit(solution)/shard_map/ppermute | solution.py:23
  46.2 10.9 %collective-permute-start.8 = (bf16[256,256]{1,0:T(8,128)(2,1)S(1)}, bf16[256,256]{1,0:T(8,128)(2,1)S(1)}, u32[]{:S(2)}, u32[]{:S(2)}) collective-permute-start(bf16[256,256]{1,0:T(8,128)(2,1)S(1)} %get-tuple-element.30), channel_id=1, source_target_pairs={{0,192},{8,200},{16,208},{24,216},{32,224},{40,232},{48,240},{56,2... | collective-permute-start | bytes 393224 | tf_op jit(solution)/shard_map/ppermute | solution.py:23
  47.8 9.3 %collective-permute-start.9 = (bf16[256,256]{1,0:T(8,128)(2,1)S(1)}, bf16[256,256]{1,0:T(8,128)(2,1)S(1)}, u32[]{:S(2)}, u32[]{:S(2)}) collective-permute-start(bf16[256,256]{1,0:T(8,128)(2,1)S(1)} %get-tuple-element.31), channel_id=1, source_target_pairs={{0,128},{8,136},{16,144},{24,152},{32,160},{40,168},{48,176},{56,1... | collective-permute-start | bytes 393224 | tf_op jit(solution)/shard_map/ppermute | solution.py:23
